TPU v7x, 32 devices: a whole 2x2x4 slice. The times are simulated.
32 devices in a mesh: dp: 8 (over y, x, core), tensor: 4 (over z).
Axes of the slice: x: 2, y: 2, z: 4, core: 2. Of those that a mesh axis runs over, the one named last changes fastest.
Arguments:
- tokens: bfloat16 [8192, 2048], P(('dp', 'tensor')), may hold values from -6 to 6
- lengths: int32 [8, 8], P('dp'), may hold values from 0 to 1024, as said below
- qkv_weight: bfloat16 [2048, 6144], P(None, 'tensor'), may hold values from -0.1875 to 0.1875
- qkv_bias: bfloat16 [6144], P('tensor'), may hold values from -3 to 3
- dense_weight: bfloat16 [2048, 2048], P('tensor'), may hold values from -0.5 to 0.5
- dense_bias: bfloat16 [2048], replicated, may hold values from -3 to 3
- up_weight: bfloat16 [2048, 8192], P(None, 'tensor'), may hold values from -0.125 to 0.125
- up_bias: bfloat16 [8192], P('tensor'), may hold values from -3 to 3
- down_weight: bfloat16 [8192, 2048], P('tensor'), may hold values from -0.125 to 0.125
- down_bias: bfloat16 [2048], replicated, may hold values from -3 to 3
- gain_attn: bfloat16 [2048], replicated, may hold values from 0.5 to 1.5
- shift_attn: bfloat16 [2048], replicated, may hold values from -3 to 3
- gain_mlp: bfloat16 [2048], replicated, may hold values from 0.5 to 1.5
- shift_mlp: bfloat16 [2048], replicated, may hold values from -3 to 3
- out_grad: bfloat16 [8192, 2048], P(('dp', 'tensor')), may hold values from -6 to 6
Outputs:
- output: bfloat16 [8192, 2048], P(('dp', 'tensor'))
- grad_tokens: float32 [8192, 2048], P(('dp', 'tensor'))
- grad_qkv_weight: float32 [2048, 6144], P(None, 'tensor')
- grad_qkv_bias: float32 [6144], P('tensor')
- grad_dense_weight: float32 [2048, 2048], P('tensor')
- grad_dense_bias: float32 [2048], replicated
- grad_up_weight: float32 [2048, 8192], P(None, 'tensor')
- grad_up_bias: float32 [8192], P('tensor')
- grad_down_weight: float32 [8192, 2048], P('tensor')
- grad_down_bias: float32 [2048], replicated
- grad_gain_attn: float32 [2048], replicated
- grad_shift_attn: float32 [2048], replicated
- grad_gain_mlp: float32 [2048], replicated
- grad_shift_mlp: float32 [2048], replicated
Inputs may be any that keep to these rules, and one draw needn't show every extreme that they name: Each row of lengths sums to 1024. In half of the rows slot 0 holds a sequence of 1024 tokens and the next 7 slots are 0. Every other pair of slots 2 b, 2 b + 1 covers the group's tokens b * 256 to (b + 1) * 256 - 1, either as one sequence of 256 tokens and a 0, or as two sequences of 64 to 192 tokens.
All inputs are finite; a program needn't handle non-finite values.
Results may differ from a plain program's by a relative error of at most 0.015.
The roundings to bfloat16 on the way count: a program that leaves them out, or rounds other values in their place, can miss the bound.
Values may be sent and summed in bfloat16 or wider, within the bound.
No kernel may reach another device: no remote copies, remote signals or barrier semaphores. Data moves between devices by JAX's collectives and lax.ppermute only.
A program may use at most 256 MiB of HBM per device.

v0:
```python
import jax
import jax.numpy as jnp
from jax import lax
from jax.sharding import PartitionSpec as P

HEAD_DIM = 128
ROT = 32
QBLK = 512


EPSILON = 1e-05
MASKED = -1e30


def standardize(row_block):
    average = jnp.mean(row_block, axis=1, keepdims=True)
    centred = row_block - average
    inverse = lax.rsqrt(jnp.mean(centred * centred, axis=1, keepdims=True) + EPSILON)
    return (centred * inverse, inverse)


def norm_back(gradient, gain_row, scaled, inverse):
    weighted = gradient * gain_row
    first_mean = jnp.mean(weighted, axis=1, keepdims=True)
    second_mean = jnp.mean(weighted * scaled, axis=1, keepdims=True)
    return inverse * (weighted - first_mean - scaled * second_mean)


def layout(lengths, group_size):
    seq_ends = jnp.cumsum(lengths)
    row_ids = jnp.arange(group_size, dtype=jnp.int32)
    passed = (seq_ends[None, :] <= row_ids[:, None]).astype(jnp.int32)
    segment = jnp.sum(passed, axis=1)
    position = row_ids - jnp.sum(passed * lengths[None, :], axis=1)
    return (segment, position)


def rotary_tables(position):
    exponents = jnp.arange(0, ROT, 2, dtype=jnp.float32) / ROT
    inv_freq = 1.0 / 10000.0**exponents
    angles = position.astype(jnp.float32)[:, None] * inv_freq[None, :]
    angles = jnp.concatenate([angles, angles], axis=1)
    return (jnp.cos(angles)[:, None, :], jnp.sin(angles)[:, None, :])


def rotate(head_part, cosine_table, sine_table):
    half_rot = ROT // 2
    leading = head_part[..., :ROT]
    turned = jnp.concatenate([-leading[..., half_rot:], leading[..., :half_rot]], axis=-1)
    return jnp.concatenate(
        [leading * cosine_table + turned * sine_table, head_part[..., ROT:]], axis=-1
    )


def rotate_back(gradient, cosine_table, sine_table):
    half_rot = ROT // 2
    leading = gradient[..., :ROT]
    with_sine = leading * sine_table
    turned = jnp.concatenate([with_sine[..., half_rot:], -with_sine[..., :half_rot]], axis=-1)
    return jnp.concatenate([leading * cosine_table + turned, gradient[..., ROT:]], axis=-1)


def gelu_exact(pre_act):
    return jax.nn.gelu(pre_act, approximate=False)


def visible(block_start, block_rows, segment, key_rows):
    query_rows = block_start + jnp.arange(block_rows, dtype=jnp.int32)
    query_segment = lax.dynamic_slice_in_dim(segment, block_start, block_rows, 0)
    return (query_segment[:, None] == segment[None, :]) & (key_rows[None, :] <= query_rows[:, None])


def attend(query_vectors, key_vectors, value_vectors, segment, block_rows):
    group_size = query_vectors.shape[0]
    key_rows = jnp.arange(group_size, dtype=jnp.int32)
    score_scale = HEAD_DIM ** (-0.5)

    def one_block(block_start):
        query_block = lax.dynamic_slice_in_dim(query_vectors, block_start, block_rows, 0)
        allowed = visible(block_start, block_rows, segment, key_rows)
        scores = (
            jnp.einsum("qhd,khd->hqk", query_block, key_vectors, preferred_element_type=jnp.float32)
            * score_scale
        )
        scores = jnp.where(allowed[None], scores, MASKED)
        row_top = jnp.max(scores, axis=2, keepdims=True)
        exponent = jnp.exp(scores - row_top)
        row_total = jnp.sum(exponent, axis=2, keepdims=True)
        weights = (exponent / row_total).astype(jnp.bfloat16)
        context = jnp.einsum(
            "hqk,khd->qhd", weights, value_vectors, preferred_element_type=jnp.float32
        )
        return (context.astype(jnp.bfloat16), (row_top + jnp.log(row_total))[:, :, 0])

    block_starts = jnp.arange(group_size // block_rows, dtype=jnp.int32) * block_rows
    context, summary = lax.map(one_block, block_starts)
    return (context.reshape(query_vectors.shape), summary)


def attend_back(
    query_vectors, key_vectors, value_vectors, segment, block_rows, summary, grad_context
):
    group_size = query_vectors.shape[0]
    key_rows = jnp.arange(group_size, dtype=jnp.int32)
    score_scale = HEAD_DIM ** (-0.5)

    def one_block(running, block_item):
        grad_keys, grad_values = running
        block_start, log_total = block_item
        query_block = lax.dynamic_slice_in_dim(query_vectors, block_start, block_rows, 0)
        grad_block = lax.dynamic_slice_in_dim(grad_context, block_start, block_rows, 0)
        allowed = visible(block_start, block_rows, segment, key_rows)
        scores = (
            jnp.einsum("qhd,khd->hqk", query_block, key_vectors, preferred_element_type=jnp.float32)
            * score_scale
        )
        scores = jnp.where(allowed[None], scores, MASKED)
        probs = jnp.exp(scores - log_total[:, :, None])
        weights = probs.astype(jnp.bfloat16)
        grad_values = grad_values + jnp.einsum(
            "hqk,qhd->khd", weights, grad_block, preferred_element_type=jnp.float32
        )
        grad_probs = jnp.einsum(
            "qhd,khd->hqk", grad_block, value_vectors, preferred_element_type=jnp.float32
        )
        spread = jnp.sum(probs * grad_probs, axis=2, keepdims=True)
        grad_scores = (probs * (grad_probs - spread)).astype(jnp.bfloat16)
        grad_query = (
            jnp.einsum("hqk,khd->qhd", grad_scores, key_vectors, preferred_element_type=jnp.float32)
            * score_scale
        )
        grad_keys = (
            grad_keys
            + jnp.einsum(
                "hqk,qhd->khd", grad_scores, query_block, preferred_element_type=jnp.float32
            )
            * score_scale
        )
        return ((grad_keys, grad_values), grad_query)

    block_starts = jnp.arange(group_size // block_rows, dtype=jnp.int32) * block_rows
    empty_grads = jnp.zeros(key_vectors.shape, jnp.float32)
    (grad_keys, grad_values), grad_queries = lax.scan(
        one_block, (empty_grads, empty_grads), (block_starts, summary)
    )
    return (grad_queries.reshape(query_vectors.shape), grad_keys, grad_values)


def shards(
    tokens,
    lengths,
    qkv_weight,
    qkv_bias,
    dense_weight,
    dense_bias,
    up_weight,
    up_bias,
    down_weight,
    down_bias,
    gain_attn,
    shift_attn,
    gain_mlp,
    shift_mlp,
    out_grad,
):
    tensor_size = lax.axis_size("tensor")
    tok_rows = tokens.shape[0]
    group_size = tok_rows * tensor_size
    block_rows = min(QBLK, group_size)
    heads_here = dense_weight.shape[0] // HEAD_DIM
    rows_own = tokens.astype(jnp.float32)
    gains = (gain_attn.astype(jnp.float32), gain_mlp.astype(jnp.float32))
    shifts = (shift_attn.astype(jnp.float32), shift_mlp.astype(jnp.float32))
    scaled_own, inverse_own = standardize(rows_own)
    normed_attn = (scaled_own * gains[0] + shifts[0]).astype(jnp.bfloat16)
    normed_mlp = (scaled_own * gains[1] + shifts[1]).astype(jnp.bfloat16)
    normed_attn, normed_mlp = (
        lax.all_gather(normed_attn, "tensor", axis=0, tiled=True),
        lax.all_gather(normed_mlp, "tensor", axis=0, tiled=True),
    )
    segment, position = layout(lengths[0], group_size)
    cosine_table, sine_table = rotary_tables(position)
    mixed_proj = jnp.dot(
        normed_attn, qkv_weight, preferred_element_type=jnp.float32
    ) + qkv_bias.astype(jnp.float32)
    mixed_proj = mixed_proj.reshape(group_size, heads_here, 3, HEAD_DIM)
    query_vectors = rotate(mixed_proj[:, :, 0], cosine_table, sine_table).astype(jnp.bfloat16)
    key_vectors = rotate(mixed_proj[:, :, 1], cosine_table, sine_table).astype(jnp.bfloat16)
    value_vectors = mixed_proj[:, :, 2].astype(jnp.bfloat16)
    context, summary = attend(query_vectors, key_vectors, value_vectors, segment, block_rows)
    context_flat = context.reshape(group_size, heads_here * HEAD_DIM)
    hidden = jnp.dot(normed_mlp, up_weight, preferred_element_type=jnp.float32) + up_bias.astype(
        jnp.float32
    )
    active = gelu_exact(hidden).astype(jnp.bfloat16)
    branches = lax.psum_scatter(
        jnp.dot(context_flat, dense_weight, preferred_element_type=jnp.float32)
        + jnp.dot(active, down_weight, preferred_element_type=jnp.float32),
        "tensor",
        scatter_dimension=0,
        tiled=True,
    )
    output = (
        rows_own + branches + dense_bias.astype(jnp.float32) + down_bias.astype(jnp.float32)
    ).astype(jnp.bfloat16)
    grad_rows = out_grad.astype(jnp.float32)
    grad_all = lax.all_gather(out_grad, "tensor", axis=0, tiled=True)
    grad_dense_bias = jnp.sum(grad_rows, axis=0)
    grad_down_bias = jnp.sum(grad_rows, axis=0)
    grad_active = jnp.dot(grad_all, down_weight.T, preferred_element_type=jnp.float32)
    grad_down_weight = jnp.dot(active.T, grad_all, preferred_element_type=jnp.float32)
    gelu_value, gelu_pull = jax.vjp(gelu_exact, hidden)
    grad_hidden = gelu_pull(grad_active)[0].astype(jnp.bfloat16)
    grad_up_bias = jnp.sum(grad_hidden, axis=0, dtype=jnp.float32)
    grad_up_weight = jnp.dot(normed_mlp.T, grad_hidden, preferred_element_type=jnp.float32)
    grad_normed_mlp = jnp.dot(grad_hidden, up_weight.T, preferred_element_type=jnp.float32)
    mlp_grads = (grad_up_weight, grad_up_bias, grad_down_weight)
    grad_context = jnp.dot(grad_all, dense_weight.T, preferred_element_type=jnp.float32).astype(
        jnp.bfloat16
    )
    grad_dense_weight = jnp.dot(context_flat.T, grad_all, preferred_element_type=jnp.float32)
    grad_context = grad_context.reshape(group_size, heads_here, HEAD_DIM)
    grad_queries, grad_keys, grad_values = attend_back(
        query_vectors, key_vectors, value_vectors, segment, block_rows, summary, grad_context
    )
    grad_mixed = jnp.stack(
        [
            rotate_back(grad_queries, cosine_table, sine_table),
            rotate_back(grad_keys, cosine_table, sine_table),
            grad_values,
        ],
        axis=2,
    )
    grad_mixed = grad_mixed.reshape(group_size, heads_here * 3 * HEAD_DIM).astype(jnp.bfloat16)
    grad_qkv_bias = jnp.sum(grad_mixed, axis=0, dtype=jnp.float32)
    grad_qkv_weight = jnp.dot(normed_attn.T, grad_mixed, preferred_element_type=jnp.float32)
    grad_normed_attn = jnp.dot(grad_mixed, qkv_weight.T, preferred_element_type=jnp.float32)
    attn_own, mlp_own = (
        lax.psum_scatter(
            grad_normed_attn.astype(jnp.bfloat16), "tensor", scatter_dimension=0, tiled=True
        ).astype(jnp.float32),
        lax.psum_scatter(
            grad_normed_mlp.astype(jnp.bfloat16), "tensor", scatter_dimension=0, tiled=True
        ).astype(jnp.float32),
    )
    gain_attn_part = jnp.sum(attn_own * scaled_own, axis=0)
    shift_attn_part = jnp.sum(attn_own, axis=0)
    gain_mlp_part = jnp.sum(mlp_own * scaled_own, axis=0)
    shift_mlp_part = jnp.sum(mlp_own, axis=0)
    grad_tokens = (
        grad_rows
        + norm_back(attn_own, gains[0], scaled_own, inverse_own)
        + norm_back(mlp_own, gains[1], scaled_own, inverse_own)
    )
    shared = lax.psum(
        (
            gain_attn_part,
            shift_attn_part,
            gain_mlp_part,
            shift_mlp_part,
            grad_dense_bias,
            grad_down_bias,
        ),
        ("dp", "tensor"),
    )
    summed = (
        lax.psum(grad_qkv_weight.astype(jnp.bfloat16), "dp").astype(jnp.float32),
        lax.psum(grad_qkv_bias.astype(jnp.bfloat16), "dp").astype(jnp.float32),
        lax.psum(grad_dense_weight.astype(jnp.bfloat16), "dp").astype(jnp.float32),
        lax.psum(mlp_grads[0].astype(jnp.bfloat16), "dp").astype(jnp.float32),
        lax.psum(mlp_grads[1].astype(jnp.bfloat16), "dp").astype(jnp.float32),
        lax.psum(mlp_grads[2].astype(jnp.bfloat16), "dp").astype(jnp.float32),
    )
    return (
        output,
        grad_tokens,
        summed[0],
        summed[1],
        summed[2],
        shared[4],
        summed[3],
        summed[4],
        summed[5],
        shared[5],
        shared[0],
        shared[1],
        shared[2],
        shared[3],
    )


def solution(mesh):
    placed = (
        P(("dp", "tensor"), None),
        P("dp", None),
        P(None, "tensor"),
        P("tensor"),
        P("tensor", None),
        P(),
        P(None, "tensor"),
        P("tensor"),
        P("tensor", None),
        P(),
        P(),
        P(),
        P(),
        P(),
        P(("dp", "tensor"), None),
    )
    return jax.shard_map(
        shards,
        mesh=mesh,
        in_specs=placed,
        out_specs=(
            P(("dp", "tensor"), None),
            P(("dp", "tensor"), None),
            P(None, "tensor"),
            P("tensor"),
            P("tensor", None),
            P(),
            P(None, "tensor"),
            P("tensor"),
            P("tensor", None),
            P(),
            P(),
            P(),
            P(),
            P(),
        ),
        check_vma=False,
    )
```

profile of v0, /device:TPU:0, one launch (start us, length us, event | category | flops | bytes accessed | tf_op | source)
XLA Modules:
  0.0 950.2 jit_solution(1985394293308734477)
XLA Ops:
  19.6 80.7 %all-gather.4.cloned.1.call-done = bf16[1024,2048]{1,0:T(8,128)(2,1)} async-done(((bf16[256,2048]{1,0:T(8,128)(2,1)}), bf16[1024,2048]{1,0:T(8,128)(2,1)}) %all-gather.4.cloned.1.call-update) | async-done | bytes 4194320 | tf_op jit(solution)/shard_map/all_gather | solution.py:178
  100.2 11.7 %convolution_add_fusion = f32[1024,1536]{1,0:T(8,128)} fusion(bf16[1024,2048]{1,0:T(8,128)(2,1)} %all-gather.4.cloned.1.call-done, bf16[2048,1536]{1,0:T(8,128)(2,1)} %param.21, f32[1536]{0:T(1024)S(1)} %convert_element_type.137), kind=kOutput, calls=%fused_computation.71 | convolution fusion | flops 6444023808 | bytes 16783360 | tf_op jit(solution)/shard_map/dot_general | solution.py:183
  111.9 6.6 copy.80
  134.6 27.3 %while.28 = (s32[]{:T(128)}, bf16[2,512,4,128]{3,2,1,0:T(4,128)(2,1)}, f32[2,4,512]{2,1,0:T(4,128)S(1)}, s32[2]{0:T(128)S(1)}, s32[1024]{0:T(1024)S(1)}, /*index...) while((s32[]{:T(128)}, ...), condition=%wide.region_8.9_spmd.clone, body=%wide.region_5.8_spmd.clone.sunk | while | flops 1100741120 | bytes 35732164 | solution.py:96
  161.9 19.2 %all-gather.8.cloned.1.call-done = bf16[1024,2048]{1,0:T(8,128)(2,1)} async-done(((bf16[256,2048]{1,0:T(8,128)(2,1)}), bf16[1024,2048]{1,0:T(8,128)(2,1)}) %all-gather.8.cloned.1.call-update) | async-done | bytes 4194320 | tf_op jit(solution)/shard_map/all_gather | solution.py:207
  181.1 5.5 convolution_convert_fusion.6
  186.6 53.5 %while.29 = (s32[]{:T(128)}, f32[1024,4,128]{0,2,1:T(8,128)}, f32[1024,4,128]{0,2,1:T(8,128)}, f32[2,512,4,128]{3,1,0,2:T(8,128)}, s32[2]{0:T(128)S(1)}, /*index...) while((s32[]{:T(128)}, f32[1024,4,128]{0,2,1:T(8,128)}, ...), condition=%wide.region_12.13_spmd.clone, body=%wide.region_10.12_spmd.clone.sunk | while | flops 2720266752 | bytes 180427744 | solution.py:143
  200.7 4.9 bitcast_add_fusion.4
  208.6 4.0 bitcast_add_fusion.5
  226.4 5.5 bitcast_add_fusion.4
  234.8 5.2 bitcast_add_fusion.5
  264.5 4.6 copy.96
  269.1 11.2 %convolution_convert_fusion.3 = bf16[1024,2048]{1,0:T(8,128)(2,1)} fusion(bf16[1024,1536]{0,1:T(8,128)(2,1)} %bitcast.115, bf16[2048,1536]{1,0:T(8,128)(2,1)} %param.21), kind=kOutput, calls=%fused_computation.73 | convolution fusion | flops 6444548096 | bytes 13631488 | tf_op jit(solution)/shard_map/dot_general | solution.py:237
  280.4 13.1 %fusion.90 = f32[1024,2048]{1,0:T(8,128)S(1)} fusion(bf16[1024,2048]{1,0:T(8,128)(2,1)} %all-gather.6.cloned.1.call-done, bf16[2048,2048]{1,0:T(8,128)(2,1)} %param.25), kind=kOutput, calls=%fused_computation.167 | convolution fusion | flops 8589934592 | bytes 20971520 | tf_op jit(solution)/shard_map/dot_general | solution.py:192
  293.6 31.4 %fusion.85 = (bf16[2048]{0:T(1024)(128)(2,1)S(1)}, bf16[1024,2048]{1,0:T(8,128)(2,1)S(1)}, f32[1024,2048]{1,0:T(8,128)}) fusion(f32[1024,2048]{1,0:T(8,128)S(1)} %fusion.90, f32[2048]{0:T(1024)S(1)} %copy-done.22, bf16[1024,2048]{1,0:T(8,128)(2,1)S(1)} %copy-done.34, bf16[2048,2048]{1,0:T(8,128)(2,1)} %param.27), kind=kOutput, calls=%fused_computation.163 | convolution fusion | flops 8745121792 | bytes 33566720 | tf_op jit(solution)/shard_map/dot_general | solution.py:210
  326.9 10.4 %convolution_convert_fusion.4 = bf16[1024,2048]{1,0:T(8,128)(2,1)} fusion(bf16[1024,2048]{1,0:T(8,128)(2,1)S(1)} %get-tuple-element.326, bf16[2048,2048]{1,0:T(8,128)(2,1)S(1)} %bitcast.121), kind=kOutput, calls=%fused_computation.74 | convolution fusion | flops 8592031744 | bytes 16777216 | tf_op jit(solution)/shard_map/dot_general | solution.py:216
  337.5 6.3 convolution_convert_fusion.5
  343.8 8.1 multiply_convert_fusion.1
  351.9 13.1 %convolution_convert_fusion.2 = bf16[2048,1536]{1,0:T(8,128)(2,1)} fusion(bf16[1024,2048]{1,0:T(8,128)(2,1)} %all-gather.4.cloned.1.call-done, bf16[1024,1536]{0,1:T(8,128)(2,1)} %bitcast.116), kind=kOutput, calls=%fused_computation.69 | convolution fusion | flops 6445596672 | bytes 13631488 | tf_op jit(solution)/shard_map/dot_general | solution.py:236
  365.0 11.4 %convolution_convert_fusion.1 = bf16[2048,2048]{1,0:T(8,128)(2,1)} fusion(bf16[1024,2048]{1,0:T(8,128)(2,1)S(1)} %copy-done.36, bf16[1024,2048]{1,0:T(8,128)(2,1)S(1)} %copy-done.38), kind=kOutput, calls=%fused_computation.68 | convolution fusion | flops 8594128896 | bytes 16777216 | tf_op jit(solution)/shard_map/dot_general | solution.py:215
  376.4 11.7 %convolution_convert_fusion = bf16[2048,2048]{1,0:T(8,128)(2,1)} fusion(bf16[1024,2048]{1,0:T(8,128)(2,1)S(1)} %multiply_convert_fusion.1, bf16[1024,2048]{1,0:T(8,128)(2,1)S(1)} %copy-done.35), kind=kOutput, calls=%fused_computation.67 | convolution fusion | flops 8594128896 | bytes 16777216 | tf_op jit(solution)/shard_map/dot_general | solution.py:211
  388.2 12.5 %fusion.91 = f32[1024,2048]{1,0:T(8,128)S(1)} fusion(bf16[1024,2048]{1,0:T(8,128)(2,1)} %copy-done.12, bf16[2048,2048]{1,0:T(8,128)(2,1)} %param.27), kind=kOutput, calls=%fused_computation.168 | convolution fusion | flops 8589934592 | bytes 20971520 | tf_op jit(solution)/shard_map/dot_general | solution.py:198
  400.7 6.9 convolution_add_fusion.1
  408.3 13.9 %all-reduce.1 = (bf16[1536]{0:T(1024)(128)(2,1)S(1)}, bf16[2048]{0:T(1024)(128)(2,1)S(1)}) all-reduce(bf16[1536]{0:T(1024)(128)(2,1)S(1)} %reduce_sum.174, bf16[2048]{0:T(1024)(128)(2,1)S(1)} %get-tuple-element.325), channel_id=1, replica_groups=mesh['dp'=8,'tensor'=4] {'dp'}, use_global_device_ids=true, to_apply=%region_21.22 | all-reduce | flops 3584 | bytes 14336 | tf_op jit(solution)/shard_map/psum | solution.py:268
  423.4 12.3 %reduce-scatter.8.cloned.1.call-done = bf16[256,2048]{1,0:T(8,128)(2,1)} async-done(((bf16[1024,2048]{1,0:T(8,128)(2,1)}), bf16[256,2048]{1,0:T(8,128)(2,1)}) %reduce-scatter.8.cloned.1.call-update) | async-done | bytes 1048592 | tf_op jit(solution)/shard_map/reduce_scatter | solution.py:242
  439.2 309.1 %all-reduce.5.cloned.1.call-done = (bf16[2048,1536]{1,0:T(8,128)(2,1)}, bf16[512,2048]{1,0:T(8,128)(2,1)}, bf16[2048,2048]{1,0:T(8,128)(2,1)}, bf16[2048,2048]{1,0:T(8,128)(2,1)}) async-done(((bf16[2048,1536]{1,0:T(8,128)(2,1)}, bf16[512,2048]{1,0:T(8,128)(2,1)}, bf16[2048,2048]{1,0:T(8,128)(2,1)}, bf16[2048,2048]{1,0:T(8,128)(2,1)}), (bf16[2048,1536]{1,0:T(8,128)(2,1)}, bf16[512,2048]{1,0:T(8,128)(2,1)}, ...) | async-done | bytes 25165840 | tf_op jit(solution)/shard_map/psum | solution.py:267
  748.3 11.8 %convert_element_type.163 = f32[2048,2048]{1,0:T(8,128)} convert(bf16[2048,2048]{1,0:T(8,128)(2,1)} %get-tuple-element.323) | non-fusion elementwise | flops 4194304 | bytes 25165824 | tf_op jit(solution)/shard_map/convert_element_type | solution.py:270
  760.2 11.7 %convert_element_type.166 = f32[2048,2048]{1,0:T(8,128)} convert(bf16[2048,2048]{1,0:T(8,128)(2,1)} %get-tuple-element.324) | non-fusion elementwise | flops 4194304 | bytes 25165824 | tf_op jit(solution)/shard_map/convert_element_type | solution.py:272
  771.8 9.5 convert_element_type.158
  783.9 111.6 %reduce-scatter.4.cloned.1.call-done = f32[256,2048]{1,0:T(8,128)} async-done(((f32[1024,2048]{1,0:T(8,128)}), f32[256,2048]{1,0:T(8,128)}) %reduce-scatter.4.cloned.1.call-update) | async-done | bytes 2097168 | tf_op jit(solution)/shard_map/reduce_scatter | solution.py:196
  895.4 5.0 convert_reduce_fusion.3
  900.4 41.9 %all-reduce = (f32[2048]{0:T(1024)S(1)}, f32[2048]{0:T(1024)}, f32[2048]{0:T(1024)}, f32[2048]{0:T(1024)}, f32[2048]{0:T(1024)}) all-reduce(f32[2048]{0:T(1024)S(1)} %get-tuple-element.342, f32[2048]{0:T(1024)S(1)} %get-tuple-element.271, f32[2048]{0:T(1024)S(1)} %get-tuple-element.272, ...), channel_id=1, replica_groups=mesh['dp'=8,'tensor'=4] {'dp','tensor'}, use_global_device_ids=true, to_apply=%region_24.25 | all-reduce | flops 10240 | bytes 81920 | tf_op jit(solution)/shard_map/psum | solution.py:255
  (214 shorter events, 116.2 us)
Async XLA Ops:
  7.2 173.9 %copy-start = (bf16[512,2048]{1,0:T(8,128)(2,1)S(1)}, bf16[512,2048]{1,0:T(8,128)(2,1)}, u32[]{:S(2)}) copy-start(bf16[512,2048]{1,0:T(8,128)(2,1)} %param.23) | copy-start | bytes 6291460
  7.2 11.0 %copy-start.29 = (bf16[1536]{0:T(1024)(128)(2,1)S(1)}, bf16[1536]{0:T(1024)(128)(2,1)}, u32[]{:S(2)}) copy-start(bf16[1536]{0:T(1024)(128)(2,1)} %param.22) | copy-start | bytes 9220
  7.2 11.1 %copy-start.33 = (s32[1,8]{1,0:T(1,128)S(1)}, s32[1,8]{1,0:T(1,128)}, u32[]{:S(2)}) copy-start(s32[1,8]{1,0:T(1,128)} %param.20) | copy-start | bytes 100
  7.2 11.7 %copy-start.30 = (bf16[2048]{0:T(1024)(128)(2,1)S(1)}, bf16[2048]{0:T(1024)(128)(2,1)}, u32[]{:S(2)}) copy-start(bf16[2048]{0:T(1024)(128)(2,1)} %param.26) | copy-start | bytes 12292
  7.2 93.0 %all-gather.4.cloned.1.call-start = ((), (), s32[]{:S(2)}) async-start(), calls=%async_computation.3 | async-start | bytes 5242880 | tf_op jit(solution)/shard_map/all_gather | solution.py:178
  8.9 7.7 copy-start.23
  16.6 164.4 %all-gather.8.cloned.1.call-start = ((), (), s32[]{:S(2)}) async-start(), calls=%async_computation.6 | async-start | bytes 5242880 | tf_op jit(solution)/shard_map/all_gather | solution.py:207
  17.4 263.0 %all-gather.6.cloned.1.call-start = ((), (), s32[]{:S(2)}) async-start(), calls=%async_computation.4 | async-start | bytes 5242880 | tf_op jit(solution)/shard_map/all_gather | solution.py:179
  18.1 405.3 %reduce-scatter.6.cloned.1.call-start = ((), (), s32[]{:S(2)}) async-start(), calls=%async_computation.7 | async-start | bytes 5242880 | tf_op jit(solution)/shard_map/reduce_scatter | solution.py:239
  18.9 106.1 %copy-start.14 = (f32[1024,32]{0,1:T(8,128)}, f32[1024,32]{0,1:T(8,128)S(1)}, u32[]{:S(2)}) copy-start(f32[1024,32]{0,1:T(8,128)S(1)} %get-tuple-element.356) | copy-start | bytes 393220
  18.9 106.1 %copy-start.16 = (f32[1024,32]{0,1:T(8,128)}, f32[1024,32]{0,1:T(8,128)S(1)}, u32[]{:S(2)}) copy-start(f32[1024,32]{0,1:T(8,128)S(1)} %get-tuple-element.355) | copy-start | bytes 393220
  226.4 7.8 copy-start.2
  240.1 7.9 copy-start.15
  240.1 9.1 copy-start.17
  280.3 13.2 %copy-start.22 = (f32[2048]{0:T(1024)S(1)}, f32[2048]{0:T(1024)}, u32[]{:S(2)}) copy-start(f32[2048]{0:T(1024)} %convert_element_type.143) | copy-start | bytes 24580
  280.3 155.4 %reduce-scatter.8.cloned.1.call-start = ((), (), s32[]{:S(2)}) async-start(), calls=%async_computation.8 | async-start | bytes 5242880 | tf_op jit(solution)/shard_map/reduce_scatter | solution.py:242
  280.4 13.1 %copy-start.34 = (bf16[1024,2048]{1,0:T(8,128)(2,1)S(1)}, bf16[1024,2048]{1,0:T(8,128)(2,1)}, u32[]{:S(2)}) copy-start(bf16[1024,2048]{1,0:T(8,128)(2,1)} %all-gather.8.cloned.1.call-done) | copy-start | bytes 12582916
  280.4 46.5 %slice-start = ((s8[8388608]{0:T(1024)(128)(4,1)}), s8[4194304]{0:T(1024)(128)(4,1)S(1)}, s32[]{:S(2)}) async-start(s8[8388608]{0:T(1024)(128)(4,1)} %bitcast.120), calls=%async_computation.10 | async-start | bytes 8388608
  293.5 31.4 %copy-start.9 = (f32[1024,2048]{1,0:T(8,128)}, f32[1024,2048]{1,0:T(8,128)S(1)}, u32[]{:S(2)}) copy-start(f32[1024,2048]{1,0:T(8,128)S(1)} %fusion.90) | copy-start | bytes 25165828
  293.5 33.3 %slice-start.1 = ((s8[8388608]{0:T(1024)(128)(4,1)}), s8[4194304]{0:T(1024)(128)(4,1)S(1)}, s32[]{:S(2)}) async-start(s8[8388608]{0:T(1024)(128)(4,1)} %bitcast.120), calls=%async_computation.11 | async-start | bytes 8388608
  337.3 411.0 %all-reduce.5.cloned.1.call-start = ((), (), s32[]{:S(2)}) async-start(), calls=%async_computation.9 | async-start | bytes 50331648 | tf_op jit(solution)/shard_map/psum | solution.py:267
  351.9 24.5 %copy-start.12 = (bf16[1024,2048]{1,0:T(8,128)(2,1)}, bf16[1024,2048]{1,0:T(8,128)(2,1)S(1)}, u32[]{:S(2)}) copy-start(bf16[1024,2048]{1,0:T(8,128)(2,1)S(1)} %multiply_convert_fusion.1) | copy-start | bytes 12582916
  351.9 13.1 %copy-start.36 = (bf16[1024,2048]{1,0:T(8,128)(2,1)S(1)}, bf16[1024,2048]{1,0:T(8,128)(2,1)}, u32[]{:S(2)}) copy-start(bf16[1024,2048]{1,0:T(8,128)(2,1)} %all-gather.6.cloned.1.call-done) | copy-start | bytes 12582916
  351.9 13.1 %copy-start.38 = (bf16[1024,2048]{1,0:T(8,128)(2,1)S(1)}, bf16[1024,2048]{1,0:T(8,128)(2,1)}, u32[]{:S(2)}) copy-start(bf16[1024,2048]{1,0:T(8,128)(2,1)} %copy-done.37) | copy-start | bytes 12582916
  365.0 11.4 %copy-start.35 = (bf16[1024,2048]{1,0:T(8,128)(2,1)S(1)}, bf16[1024,2048]{1,0:T(8,128)(2,1)}, u32[]{:S(2)}) copy-start(bf16[1024,2048]{1,0:T(8,128)(2,1)} %all-gather.8.cloned.1.call-done) | copy-start | bytes 12582916
  388.1 507.3 %reduce-scatter.4.cloned.1.call-start = ((), (), s32[]{:S(2)}) async-start(), calls=%async_computation.5 | async-start | bytes 10485760 | tf_op jit(solution)/shard_map/reduce_scatter | solution.py:196
  407.6 28.1 %copy-start.8 = (bf16[256,2048]{1,0:T(8,128)(2,1)S(1)}, bf16[256,2048]{1,0:T(8,128)(2,1)}, u32[]{:S(2)}) copy-start(bf16[256,2048]{1,0:T(8,128)(2,1)} %param.19) | copy-start | bytes 3145732
  407.6 28.1 %copy-start.19 = (f32[2048]{0:T(1024)S(1)}, f32[2048]{0:T(1024)}, u32[]{:S(2)}) copy-start(f32[2048]{0:T(1024)} %copy-done.18) | copy-start | bytes 24580
  407.6 28.1 %copy-start.21 = (f32[2048]{0:T(1024)S(1)}, f32[2048]{0:T(1024)}, u32[]{:S(2)}) copy-start(f32[2048]{0:T(1024)} %copy-done.20) | copy-start | bytes 24580
  407.6 28.1 %copy-start.24 = (f32[256]{0:T(256)S(1)}, f32[256]{0:T(256)}, u32[]{:S(2)}) copy-start(f32[256]{0:T(256)} %copy-done.23) | copy-start | bytes 3076
  407.6 28.1 %copy-start.26 = (f32[256]{0:T(256)S(1)}, f32[256]{0:T(256)}, u32[]{:S(2)}) copy-start(f32[256]{0:T(256)} %copy-done.25) | copy-start | bytes 3076
  771.8 9.5 copy-start.13
  (25 other events, 86.1 us)
Sparse Core Ops, SparseCore 0:
  16.7 83.4 all-gather.3
  101.8 79.2 all-gather.7
  182.6 79.2 all-gather.5
  280.4 75.1 reduce-scatter.5
  358.4 77.2 reduce-scatter.7
  440.9 307.3 all-reduce.4
  750.7 144.7 reduce-scatter.3
where the time goes:
time: 961 us; the launch traced here: 950 us
  waiting for transfers between devices  534 us (56%)
  matrix products  194 us (20%)
  other arithmetic  94.2 us (10%)
  blocking collectives  55.8 us (6%)
  local copies, waits for them, and re-layouts  48.3 us (5%)
  between operations  15.1 us (2%)
    psum x1, waiting for transfers between devices, shards(): lax.psum(grad_qkv_weight.astype(jnp.bfloat16), 'dp').astype(jnp.float32)  309 us
    reduce_scatter x1, waiting for transfers between devices, shards(): lax.psum_scatter(jnp.dot(context_flat, dense_weight, preferred_element_ty...  112 us
    all_gather x1, waiting for transfers between devices, shards(): lax.all_gather(normed_attn, 'tensor', axis=0, tiled=True)  80.7 us
    psum x1, blocking collectives, shards(): lax.psum((gain_attn_part, shift_attn_part, gain_mlp_part, shift_mlp_part,...  41.9 us
    dot_general x1, matrix products, shards(): jnp.dot(grad_all, down_weight.T, preferred_element_type=jnp.float32)  31.4 us
  transfers between devices with their start and end apart: 7, of which 5 were waited for; matrix products, arithmetic and copies ran while one was open for 33% of the time, Pallas kernels for 0%

commit v1 on v0

v1 whole, which is shorter than its diff:
```python
import jax
import jax.numpy as jnp
from jax import lax
from jax.experimental import pallas as pl
from jax.experimental.pallas import tpu as pltpu
from jax.sharding import PartitionSpec as P

HEAD_DIM = 128
ROT = 32
EPSILON = 1e-05
MASKED = -1e30
BF16 = jnp.bfloat16
F32 = jnp.float32


def standardize(row_block):
    average = jnp.mean(row_block, axis=1, keepdims=True)
    centred = row_block - average
    inverse = lax.rsqrt(jnp.mean(centred * centred, axis=1, keepdims=True) + EPSILON)
    return (centred * inverse, inverse)


def layout(lengths, group_size):
    seq_ends = jnp.cumsum(lengths)
    row_ids = jnp.arange(group_size, dtype=jnp.int32)
    passed = (seq_ends[None, :] <= row_ids[:, None]).astype(jnp.int32)
    first_row = jnp.sum(passed * lengths[None, :], axis=1)
    return (first_row, row_ids - first_row)


def rotary_tables(position):
    exponents = jnp.arange(0, ROT, 2, dtype=F32) / ROT
    inv_freq = 1.0 / 10000.0**exponents
    angles = position.astype(F32)[:, None] * inv_freq[None, :]
    cosine, sine = jnp.cos(angles), jnp.sin(angles)
    rows, half = angles.shape
    keep = jnp.concatenate([cosine, cosine, jnp.ones((rows, HEAD_DIM - ROT), F32)], axis=1)
    low = jnp.concatenate([-sine, jnp.zeros((rows, HEAD_DIM - half), F32)], axis=1)
    high = jnp.concatenate(
        [jnp.zeros((rows, half), F32), sine, jnp.zeros((rows, HEAD_DIM - ROT), F32)], axis=1
    )
    return (keep, low, high)


def turn(u, keep, low, high):
    return (
        u * keep
        + pltpu.roll(u, HEAD_DIM - ROT // 2, 1) * low
        + pltpu.roll(u, ROT // 2, 1) * high
    )


def turn_back(u, keep, low, high):
    return (
        u * keep
        - pltpu.roll(u, HEAD_DIM - ROT // 2, 1) * low
        - pltpu.roll(u, ROT // 2, 1) * high
    )


def dot_nt(a, b):
    return lax.dot_general(a, b, (((1,), (1,)), ((), ())), preferred_element_type=F32)


def dot_tn(a, b):
    return lax.dot_general(a, b, (((0,), (0,)), ((), ())), preferred_element_type=F32)


def dot_nn(a, b):
    return jnp.dot(a, b, preferred_element_type=F32)


def attend_kernel(blocks, place_ref, mixed_ref, keep_ref, low_ref, high_ref, first_ref, qkv_ref, context_ref):
    rows = mixed_ref.shape[0] // blocks
    scale = HEAD_DIM ** (-0.5)

    def slot(i):
        return pl.ds(pl.multiple_of(lax.rem(place_ref[0] - i + blocks, blocks) * rows, rows), rows)

    for i in range(blocks):
        here = slice(i * rows, (i + 1) * rows)
        tables = (keep_ref[here, :], low_ref[here, :], high_ref[here, :])
        there = slot(i)
        qkv_ref[here, 0:128] = turn(mixed_ref[there, 0:128], *tables).astype(BF16)
        qkv_ref[here, 128:256] = turn(mixed_ref[there, 128:256], *tables).astype(BF16)
        qkv_ref[here, 256:384] = mixed_ref[there, 256:384].astype(BF16)
    for i in range(blocks):
        count = (i + 1) * rows
        query = qkv_ref[i * rows : count, 0:128]
        scores = dot_nt(query, qkv_ref[0:count, 128:256]) * scale
        key_at = lax.broadcasted_iota(jnp.int32, scores.shape, 1)
        query_at = lax.broadcasted_iota(jnp.int32, scores.shape, 0) + i * rows
        seen = (key_at >= first_ref[i * rows : count, :]) & (key_at <= query_at)
        scores = jnp.where(seen, scores, MASKED)
        top = jnp.max(scores, axis=1, keepdims=True)
        raised = jnp.exp(scores - top)
        total = jnp.sum(raised, axis=1, keepdims=True)
        weights = (raised * (1.0 / total)).astype(BF16)
        context_ref[slot(i), :] = dot_nn(weights, qkv_ref[0:count, 256:384]).astype(BF16)


def attend(mixed, tables, first_row, place, blocks):
    group, width = mixed.shape
    heads = width // (3 * HEAD_DIM)
    whole = lambda h, p: (0, 0)
    by_head = lambda h, p: (0, h)
    table = pl.BlockSpec((group, HEAD_DIM), whole)
    return pl.pallas_call(
        lambda *refs: attend_kernel(blocks, *refs),
        out_shape=(
            jax.ShapeDtypeStruct((group, width), BF16),
            jax.ShapeDtypeStruct((group, heads * HEAD_DIM), BF16),
        ),
        grid_spec=pltpu.PrefetchScalarGridSpec(
            num_scalar_prefetch=1,
            grid=(heads,),
            in_specs=[
                pl.BlockSpec((group, 3 * HEAD_DIM), by_head),
                table,
                table,
                table,
                pl.BlockSpec((group, 1), whole),
            ],
            out_specs=(
                pl.BlockSpec((group, 3 * HEAD_DIM), by_head),
                pl.BlockSpec((group, HEAD_DIM), by_head),
            ),
        ),
        compiler_params=pltpu.CompilerParams(dimension_semantics=("arbitrary",)),
        name="attend",
    )(place, mixed, *tables, first_row[:, None])


def attend_back_kernel(
    blocks,
    place_ref,
    qkv_ref,
    grad_ref,
    keep_ref,
    low_ref,
    high_ref,
    first_ref,
    mixed_ref,
    sums_ref,
    keys_ref,
    values_ref,
):
    rows = qkv_ref.shape[0] // blocks
    scale = HEAD_DIM ** (-0.5)

    def slot(i):
        return pl.ds(pl.multiple_of(lax.rem(place_ref[0] - i + blocks, blocks) * rows, rows), rows)

    def tables(i):
        here = slice(i * rows, (i + 1) * rows)
        return (keep_ref[here, :], low_ref[here, :], high_ref[here, :])

    query_sum = jnp.zeros((1, HEAD_DIM), F32)
    key_sum = jnp.zeros((1, HEAD_DIM), F32)
    value_sum = jnp.zeros((1, HEAD_DIM), F32)
    for i in reversed(range(blocks)):
        count = (i + 1) * rows
        query = qkv_ref[i * rows : count, 0:128]
        keys = qkv_ref[0:count, 128:256]
        grad = grad_ref[slot(i), :]
        scores = dot_nt(keys, query) * scale
        key_at = lax.broadcasted_iota(jnp.int32, scores.shape, 0)
        query_at = lax.broadcasted_iota(jnp.int32, scores.shape, 1) + i * rows
        seen = (key_at >= first_ref[:, i * rows : count]) & (key_at <= query_at)
        scores = jnp.where(seen, scores, MASKED)
        top = jnp.max(scores, axis=0, keepdims=True)
        raised = jnp.exp(scores - top)
        total = jnp.sum(raised, axis=0, keepdims=True)
        probs = raised * (1.0 / total)
        grad_values = dot_nn(probs.astype(BF16), grad)
        grad_probs = dot_nt(qkv_ref[0:count, 256:384], grad)
        spread = jnp.sum(probs * grad_probs, axis=0, keepdims=True)
        grad_scores = (probs * (grad_probs - spread)).astype(BF16)
        grad_keys = dot_nn(grad_scores, query)
        if i == blocks - 1:
            values_ref[...] = grad_values
            keys_ref[...] = grad_keys
        else:
            values_ref[0:count, :] += grad_values
            keys_ref[0:count, :] += grad_keys
        grad_query = turn_back(dot_tn(grad_scores, keys) * scale, *tables(i)).astype(BF16)
        mixed_ref[slot(i), 0:128] = grad_query
        query_sum += jnp.sum(grad_query.astype(F32), axis=0, keepdims=True)
        here = slice(i * rows, count)
        if i == 0:
            for j in range(blocks):
                here = slice(j * rows, (j + 1) * rows)
                grad_key = turn_back(keys_ref[here, :] * scale, *tables(j)).astype(BF16)
                grad_value = values_ref[here, :].astype(BF16)
                mixed_ref[slot(j), 128:256] = grad_key
                mixed_ref[slot(j), 256:384] = grad_value
                key_sum += jnp.sum(grad_key.astype(F32), axis=0, keepdims=True)
                value_sum += jnp.sum(grad_value.astype(F32), axis=0, keepdims=True)
    sums_ref[:, 0:128] = jnp.broadcast_to(query_sum, (8, HEAD_DIM))
    sums_ref[:, 128:256] = jnp.broadcast_to(key_sum, (8, HEAD_DIM))
    sums_ref[:, 256:384] = jnp.broadcast_to(value_sum, (8, HEAD_DIM))


def attend_back(qkv, grad_context, tables, first_row, place, blocks):
    group, width = qkv.shape
    heads = width // (3 * HEAD_DIM)
    whole = lambda h, p: (0, 0)
    by_head = lambda h, p: (0, h)
    table = pl.BlockSpec((group, HEAD_DIM), whole)
    mixed, sums = pl.pallas_call(
        lambda *refs: attend_back_kernel(blocks, *refs),
        out_shape=(
            jax.ShapeDtypeStruct((group, width), BF16),
            jax.ShapeDtypeStruct((8, width), F32),
        ),
        grid_spec=pltpu.PrefetchScalarGridSpec(
            num_scalar_prefetch=1,
            grid=(heads,),
            in_specs=[
                pl.BlockSpec((group, 3 * HEAD_DIM), by_head),
                pl.BlockSpec((group, HEAD_DIM), by_head),
                table,
                table,
                table,
                pl.BlockSpec((1, group), whole),
            ],
            out_specs=(
                pl.BlockSpec((group, 3 * HEAD_DIM), by_head),
                pl.BlockSpec((8, 3 * HEAD_DIM), by_head),
            ),
            scratch_shapes=[pltpu.VMEM((group, HEAD_DIM), F32)] * 2,
        ),
        compiler_params=pltpu.CompilerParams(dimension_semantics=("arbitrary",)),
        name="attend_back",
    )(place, qkv, grad_context, *tables, first_row[None, :])
    return (mixed, sums[0])


def after(value, *earlier):
    return lax.optimization_barrier((value, *earlier))[0]


def line_gather(own, size):
    ups, downs = [own], [own]
    for step in range(1, size):
        ups.append(
            lax.ppermute(ups[-1], "tensor", [(i, i + 1) for i in range(step - 1, size - 1)])
        )
        downs.append(
            lax.ppermute(downs[-1], "tensor", [(i, i - 1) for i in range(1, size - step + 1)])
        )
    return [own] + [ups[k] + downs[size - k] for k in range(1, size)]


def line_scatter(partial, size):
    rows = partial.shape[0] // size

    def for_ahead(k):
        at = (size - k) % size
        return partial[at * rows : (at + 1) * rows].astype(F32)

    down = up = None
    for step in range(1, size):
        send_down, send_up = for_ahead(step), for_ahead(size - step)
        if step > 1:
            send_down, send_up = send_down + down.astype(F32), send_up + up.astype(F32)
        down = lax.ppermute(
            send_down.astype(BF16), "tensor", [(i, i - 1) for i in range(size - step, size)]
        )
        up = lax.ppermute(send_up.astype(BF16), "tensor", [(i, i + 1) for i in range(step)])
    return for_ahead(0) + down.astype(F32) + up.astype(F32)


class Groups:
    def __init__(self):
        self.size = lax.axis_size("dp")
        self.bits = self.size.bit_length() - 1
        me = lax.axis_index("dp")
        self.side = [(me >> b) & 1 for b in range(self.bits)]

    def swap(self, value, bit):
        return lax.ppermute(value, "dp", [(i, i ^ (1 << bit)) for i in range(self.size)])

    def halves(self, value, bit):
        half = value.shape[0] // 2
        keep = lax.dynamic_slice_in_dim(value, self.side[bit] * half, half, 0)
        give = lax.dynamic_slice_in_dim(value, (1 - self.side[bit]) * half, half, 0)
        return keep, give

    def join(self, mine, theirs, bit):
        first = self.side[bit] == 0
        return jnp.concatenate(
            [jnp.where(first, mine, theirs), jnp.where(first, theirs, mine)], axis=0
        )

    def reduce(self, value, order):
        for bit in order:
            keep, give = self.halves(value, bit)
            value = (keep.astype(F32) + self.swap(give, bit).astype(F32)).astype(BF16)
        return value

    def gather(self, value, order):
        for bit in reversed(order):
            value = self.join(value, self.swap(value, bit), bit)
        return value

    def weight_grad(self, left, right):
        half = left.shape[1] // 2
        mine = lax.dynamic_slice_in_dim(left, self.side[0] * half, half, 1)
        other = lax.dynamic_slice_in_dim(left, (1 - self.side[0]) * half, half, 1)
        came = self.swap(dot_tn(other, right).astype(BF16), 0)
        both = (dot_tn(mine, right) + came.astype(F32)).astype(BF16)
        order = list(range(1, self.bits))
        other_order = order[1:] + order[:1]
        part_a, part_b = both[: half // 2], both[half // 2 :]
        done_a, done_b = self.reduce(part_a, order), self.reduce(part_b, other_order)
        done = jnp.concatenate(
            [self.gather(done_a, order), self.gather(done_b, other_order)], axis=0
        )
        return self.join(done, self.swap(done, 0), 0).astype(F32)

    def small_sum(self, value):
        for bit in range(self.bits):
            value = value + self.swap(value, bit)
        return value


def line_sum(value, size):
    reach = 1
    while reach < size:
        value = value + lax.ppermute(value, "tensor", [(i, i ^ reach) for i in range(size)])
        reach *= 2
    return value


def shards(
    tokens,
    lengths,
    qkv_weight,
    qkv_bias,
    dense_weight,
    dense_bias,
    up_weight,
    up_bias,
    down_weight,
    down_bias,
    gain_attn,
    shift_attn,
    gain_mlp,
    shift_mlp,
    out_grad,
):
    size = lax.axis_size("tensor")
    group_size = tokens.shape[0] * size
    place = lax.axis_index("tensor").astype(jnp.int32)[None]
    groups = Groups()
    gains = (gain_attn.astype(F32), gain_mlp.astype(F32))
    shifts = (shift_attn.astype(F32), shift_mlp.astype(F32))
    first_row, position = layout(lengths[0], group_size)
    tables = rotary_tables(position)

    rows = jnp.concatenate(line_gather(tokens, size), axis=0)
    grad_all = jnp.concatenate(line_gather(after(out_grad, rows), size), axis=0)

    scaled, inverse = standardize(rows.astype(F32))
    normed_attn = (scaled * gains[0] + shifts[0]).astype(BF16)
    normed_mlp = (scaled * gains[1] + shifts[1]).astype(BF16)
    hidden = dot_nn(normed_mlp, up_weight) + up_bias.astype(F32)
    below = 0.5 * (1.0 + lax.erf(hidden * 0.5**0.5))
    active = (hidden * below).astype(BF16)
    slope = below + hidden * jnp.exp(-0.5 * hidden * hidden) * (2.0 * jnp.pi) ** -0.5
    mixed = dot_nn(normed_attn, qkv_weight) + qkv_bias.astype(F32)
    qkv, context = attend(mixed, tables, first_row, place, size)
    partial = (dot_nn(context, dense_weight) + dot_nn(active, down_weight)).astype(BF16)
    branches = line_scatter(partial, size)
    tokens_own = tokens.astype(F32)
    output = (
        tokens_own + branches + dense_bias.astype(F32) + down_bias.astype(F32)
    ).astype(BF16)

    grad_rows = out_grad.astype(F32)
    bias_part = jnp.sum(grad_rows, axis=0)
    grad_down_weight = groups.weight_grad(active, grad_all)
    grad_hidden = (dot_nt(grad_all, down_weight) * slope).astype(BF16)
    up_bias_part = jnp.sum(grad_hidden, axis=0, dtype=F32)
    grad_up_weight = groups.weight_grad(normed_mlp, grad_hidden)
    grad_context = dot_nt(grad_all, dense_weight).astype(BF16)
    grad_dense_weight = groups.weight_grad(context, grad_all)
    grad_mixed, qkv_bias_part = attend_back(qkv, grad_context, tables, first_row, place, size)
    grad_qkv_weight = groups.weight_grad(normed_attn, grad_mixed)
    mlp_grad = dot_nt(grad_hidden, up_weight)
    attn_grad = dot_nt(grad_mixed, qkv_weight)
    inner = (mlp_grad * gains[1] + attn_grad * gains[0]).astype(BF16)
    inner_own = line_scatter(inner, size)
    scaled_own, inverse_own = standardize(tokens_own)
    grad_tokens = grad_rows + inverse_own * (
        inner_own
        - jnp.mean(inner_own, axis=1, keepdims=True)
        - scaled_own * jnp.mean(inner_own * scaled_own, axis=1, keepdims=True)
    )

    width = tokens.shape[1]
    shared = groups.small_sum(
        jnp.concatenate(
            [
                jnp.sum(attn_grad * scaled, axis=0),
                jnp.sum(attn_grad, axis=0),
                jnp.sum(mlp_grad * scaled, axis=0),
                jnp.sum(mlp_grad, axis=0),
                bias_part,
                up_bias_part,
                qkv_bias_part,
            ]
        )
    )
    split = 5 * width
    everywhere = line_sum(shared[:split], size)
    gain_attn_sum, shift_attn_sum, gain_mlp_sum, shift_mlp_sum, bias_sum = (
        everywhere[k * width : (k + 1) * width] for k in range(5)
    )
    grad_up_bias = shared[split : split + up_bias.shape[0]]
    grad_qkv_bias = shared[split + up_bias.shape[0] :]
    return (
        output,
        grad_tokens,
        grad_qkv_weight,
        grad_qkv_bias,
        grad_dense_weight,
        bias_sum,
        grad_up_weight,
        grad_up_bias,
        grad_down_weight,
        bias_sum,
        gain_attn_sum,
        shift_attn_sum,
        gain_mlp_sum,
        shift_mlp_sum,
    )


def solution(mesh):
    rows = P(("dp", "tensor"), None)
    columns = P(None, "tensor")
    return jax.shard_map(
        shards,
        mesh=mesh,
        in_specs=(
            rows,
            P("dp", None),
            columns,
            P("tensor"),
            P("tensor", None),
            P(),
            columns,
            P("tensor"),
            P("tensor", None),
            P(),
            P(),
            P(),
            P(),
            P(),
            rows,
        ),
        out_specs=(
            rows,
            rows,
            columns,
            P("tensor"),
            P("tensor", None),
            P(),
            columns,
            P("tensor"),
            P("tensor", None),
            P(),
            P(),
            P(),
            P(),
            P(),
        ),
        check_vma=False,
    )
```

time: 961 us -> 705 us (0.73)
  waiting for transfers between devices: 534 us -> 311 us
  starting transfers between devices: 0.45 us -> 98.6 us
  blocking collectives: 55.8 us -> 0 us
  matrix products: 194 us -> 141 us
  local copies, waits for them, and re-layouts: 48.3 us -> 11.4 us
  Pallas kernels: 0 us -> 33.3 us
  between operations: 15.1 us -> 2.37 us
    ppermute x0 -> x69, waiting for transfers between devices: none -> 311 us  [the longest x43 193 us: swap(): lax.ppermute(value, 'dp', [(i, i ^ 1 << bit) for i in range(self.size)])]
    psum x1 -> x0, waiting for transfers between devices: 309 us -> none  [shards(): lax.psum(grad_qkv_weight.astype(jnp.bfloat16), 'dp').astype(jnp.float32)]
    reduce_scatter x3 -> x0, waiting for transfers between devices: 124 us -> none  [the longest x1 112 us: shards(): lax.psum_scatter(jnp.dot(context_flat, dense_weight, preferred_element_ty...]
    all_gather x3 -> x0, waiting for transfers between devices: 99.9 us -> none  [the longest x1 80.7 us: shards(): lax.all_gather(normed_attn, 'tensor', axis=0, tiled=True)]
    ppermute x0 -> x69, starting transfers between devices: none -> 98.6 us  [the longest x43 39 us: swap(): lax.ppermute(value, 'dp', [(i, i ^ 1 << bit) for i in range(self.size)])]
    psum x2 -> x0, blocking collectives: 55.8 us -> none  [the longest x1 41.9 us: shards(): lax.psum((gain_attn_part, shift_attn_part, gain_mlp_part, shift_mlp_part,...]
    dot_general x26 -> x16, matrix products: 194 us -> 141 us  [the longest x4 54.9 us: dot_nt(): lax.dot_general(a, b, (((1,), (1,)), ((), ())), preferred_element_type=F32)]
    pallas_call x0 -> x2, Pallas kernels: none -> 33.3 us  [the longest x1 18.1 us: attend_back(): pl.pallas_call(lambda *refs: attend_back_kernel(blocks, *refs), out_shape...]
  transfers between devices with their start and end apart: 7 -> 69, of which waited for: 5 -> 32; matrix products, arithmetic and copies ran while one was open for 33% -> 33% of each run, Pallas kernels for 0% -> 5%
where the time goes in v1:
time: 705 us; the launch traced here: 700 us
  waiting for transfers between devices  311 us (44%)
  matrix products  141 us (20%)
  other arithmetic  102 us (14%)
  starting transfers between devices  98.6 us (14%)
  Pallas kernels  33.3 us (5%)
  local copies, waits for them, and re-layouts  11.4 us (2%)
    ppermute x43, waiting for transfers between devices, swap(): lax.ppermute(value, 'dp', [(i, i ^ 1 << bit) for i in range(self.size)])  193 us
    dot_general x4, matrix products, dot_nt(): lax.dot_general(a, b, (((1,), (1,)), ((), ())), preferred_element_type=F32)  54.9 us
    dot_general x8, matrix products, dot_tn(): lax.dot_general(a, b, (((0,), (0,)), ((), ())), preferred_element_type=F32)  44.2 us
    dot_general x4, matrix products, dot_nn(): return jnp.dot(a, b, preferred_element_type=F32)  41.7 us
    ppermute x43, starting transfers between devices, swap(): lax.ppermute(value, 'dp', [(i, i ^ 1 << bit) for i in range(self.size)])  39 us
    ppermute x6, waiting for transfers between devices, line_gather(): lax.ppermute(downs[-1], 'tensor', [(i, i - 1) for i in range(1, size - st...  35.5 us
    ppermute x6, waiting for transfers between devices, line_scatter(): lax.ppermute(send_up.astype(BF16), 'tensor', [(i, i + 1) for i in range(s...  35.3 us
    convert_element_type x4, other arithmetic, weight_grad(): return self.join(done, self.swap(done, 0), 0).astype(F32)  32.9 us
  transfers between devices with their start and end apart: 69, of which 32 were waited for; matrix products, arithmetic and copies ran while one was open for 33% of the time, Pallas kernels for 5%

profile of v1, /device:TPU:0, one launch (start us, length us, event | category | flops | bytes accessed | tf_op | source)
XLA Modules:
  0.0 699.6 jit_solution(9265258378896566957)
XLA Ops:
  7.1 21.3 %collective-permute-done = bf16[256,2048]{1,0:T(8,128)(2,1)S(1)} collective-permute-done((bf16[256,2048]{1,0:T(8,128)(2,1)}, bf16[256,2048]{1,0:T(8,128)(2,1)S(1)}, u32[]{:S(2)}, u32[]{:S(2)}) %collective-permute-start) | collective-permute-done | bytes 1048608 | tf_op jit(solution)/shard_map/ppermute | solution.py:247
  35.5 24.8 %collective-permute-done.2 = bf16[256,2048]{1,0:T(8,128)(2,1)} collective-permute-done((bf16[256,2048]{1,0:T(8,128)(2,1)S(1)}, bf16[256,2048]{1,0:T(8,128)(2,1)}, u32[]{:S(2)}, u32[]{:S(2)}) %collective-permute-start.2) | collective-permute-done | bytes 1048608 | tf_op jit(solution)/shard_map/ppermute | solution.py:250
  76.4 9.2 %collective-permute-done.3 = bf16[256,2048]{1,0:T(8,128)(2,1)} collective-permute-done((bf16[256,2048]{1,0:T(8,128)(2,1)}, bf16[256,2048]{1,0:T(8,128)(2,1)}, u32[]{:S(2)}, u32[]{:S(2)}) %collective-permute-start.3) | collective-permute-done | bytes 1048608 | tf_op jit(solution)/shard_map/ppermute | solution.py:250
  96.8 12.5 %multiply_convert_fusion = (bf16[1024,2048]{1,0:T(8,128)(2,1)}, f32[1024,2048]{1,0:T(8,128)}) fusion(f32[2048]{0:T(1024)S(1)} %convert_element_type.364, bf16[1024,2048]{1,0:T(8,128)(2,1)S(1)} %get-tuple-element.42, bf16[2048,2048]{1,0:T(8,128)(2,1)S(1)} %bitcast.32), kind=kOutput, calls=%fused_computation.29 | convolution fusion | flops 8602517504 | bytes 25174016 | tf_op jit(solution)/shard_map/dot_general | solution.py:70
  109.3 12.8 %fusion.68 = f32[1024,2048]{1,0:T(8,128)} fusion(bf16[1024,2048]{1,0:T(8,128)(2,1)} %get-tuple-element.108, bf16[2048,2048]{1,0:T(8,128)(2,1)S(1)} %bitcast.30), kind=kOutput, calls=%fused_computation.209 | convolution fusion | flops 8589934592 | bytes 20971520 | tf_op jit(solution)/shard_map/dot_general | solution.py:70
  122.1 10.4 %convolution_add_fusion.refs_1_ = f32[1024,1536]{1,0:T(8,128)} fusion(bf16[1024,2048]{1,0:T(8,128)(2,1)S(1)} %get-tuple-element.41, bf16[2048,1536]{1,0:T(8,128)(2,1)} %param.17, f32[1536]{0:T(1024)S(1)} %convert_element_type.359), kind=kOutput, calls=%fused_computation.33 | convolution fusion | flops 6444023808 | bytes 16783360 | tf_op jit(solution)/shard_map/dot_general | solution.py:70
  132.5 15.2 %attend.1 = (bf16[1024,1536]{1,0:T(8,128)(2,1)}, bf16[1024,512]{1,0:T(8,128)(2,1)}) custom-call(s32[1]{0:T(128)} %bitcast.refs_0_, f32[1024,1536]{1,0:T(8,128)} %convolution_add_fusion.refs_1_, f32[1024,128]{1,0:T(8,128)} %get-tuple-element.112.refs_2_.refs_3_, f32[1024,128]{1,0:T(8,128)} %concatenate.68.refs_3_.refs_4_, ...), custom_call_target="tpu_custom_call" | custom-call | tf_op jit(solution)/shard_map/attend/pallas_call | solution.py:108
  162.5 16.2 %collective-permute-done.9 = bf16[256,2048]{1,0:T(8,128)(2,1)S(1)} collective-permute-done((bf16[256,2048]{1,0:T(8,128)(2,1)S(1)}, bf16[256,2048]{1,0:T(8,128)(2,1)S(1)}, u32[]{:S(2)}, u32[]{:S(2)}) %collective-permute-start.9) | collective-permute-done | bytes 1048608 | tf_op jit(solution)/shard_map/ppermute | solution.py:270
  190.9 14.1 %collective-permute-done.10 = bf16[256,2048]{1,0:T(8,128)(2,1)} collective-permute-done((bf16[256,2048]{1,0:T(8,128)(2,1)}, bf16[256,2048]{1,0:T(8,128)(2,1)}, u32[]{:S(2)}, u32[]{:S(2)}) %collective-permute-start.10) | collective-permute-done | bytes 1048608 | tf_op jit(solution)/shard_map/ppermute | solution.py:270
  226.8 18.1 %attend_back.1 = (bf16[1024,1536]{1,0:T(8,128)(2,1)}, f32[8,1536]{1,0:T(8,128)}) custom-call(s32[1]{0:T(128)} %bitcast.refs_0_, bf16[1024,1536]{1,0:T(8,128)(2,1)} %get-tuple-element.21.refs_1_, bf16[1024,512]{1,0:T(8,128)(2,1)} %convolution_convert_fusion.4.refs_2_, f32[1024,128]{1,0:T(8,128)} %get-tuple-element.112.refs_2_.refs_3_, ...), custom_call_target="tpu_custom_call" | custom-call | tf_op jit(solution)/shard_map/attend_back/pallas_call | solution.py:210
  244.9 11.9 %fusion.69 = f32[1024,2048]{1,0:T(8,128)} fusion(bf16[1024,1536]{1,0:T(8,128)(2,1)} %get-tuple-element.22, bf16[2048,1536]{1,0:T(8,128)(2,1)} %param.17), kind=kOutput, calls=%fused_computation.210 | convolution fusion | flops 6442450944 | bytes 17825792 | tf_op jit(solution)/shard_map/dot_general | solution.py:62
  261.7 7.9 %convolution_convert_fusion.1 = bf16[1024,2048]{1,0:T(8,128)(2,1)} fusion(bf16[1024,2048]{1,0:T(8,128)(2,1)S(1)} %copy-done.38, s32[]{:T(128)S(6)} %select_n.290, bf16[256,2048]{1,0:T(8,128)(2,1)S(1)} %copy-done.18, bf16[256,2048]{1,0:T(8,128)(2,1)S(1)} %add.332, bf16[256,2048]{1,0:T(8,128)(2,1)S(1)} %copy-done.21, bf16[256,2048]{1,0:T(8,128)(2,1)} %param.29), kind=kOutput, calls=%fused_computation.43 | convolution fusion | flops 4313841664 | bytes 10485764 | tf_op jit(solution)/shard_map/dot_general | solution.py:66
  269.6 20.1 %convert_reduce_fusion.1 = (f32[2048]{0:T(1024)S(1)}, bf16[1024,2048]{1,0:T(8,128)(2,1)}) fusion(f32[1024,2048]{1,0:T(8,128)} %get-tuple-element.109, f32[2048]{0:T(1024)S(1)} %convert_element_type.364, bf16[2048,2048]{1,0:T(8,128)(2,1)} %param.23, bf16[256,2048]{1,0:T(8,128)(2,1)S(1)} %copy-done.18, bf16[256,2048]{1,0:T(8,128)(2,1)} %copy-done.15, ...), kind=kOutput, calls=%fused_computation.26 | convolution fusion | flops 8633972736 | bytes 25182208 | tf_op jit(solution)/shard_map/dot_general | solution.py:62
  289.7 18.0 %fusion.59 = (f32[2048]{0:T(1024)S(1)}, f32[2048]{0:T(1024)S(1)}, bf16[1024,2048]{1,0:T(8,128)(2,1)}, f32[2048]{0:T(1024)S(1)}, f32[2048]{0:T(1024)S(1)}) fusion(f32[1024]{0:T(1024)S(1)} %add_rsqrt_fusion, f32[1024]{0:T(1024)S(1)} %broadcast_multiply_fusion, bf16[1024,2048]{1,0:T(8,128)(2,1)S(1)} %copy-done.3, f32[1024,2048]{1,0:T(8,128)} %fusion.69, ...), kind=kOutput, calls=%fused_computation.200 | convolution fusion | flops 8617189376 | bytes 29417472 | tf_op jit(solution)/shard_map/dot_general | solution.py:62
  385.1 14.8 %collective-permute-done.20 = bf16[256,2048]{1,0:T(8,128)(2,1)S(1)} collective-permute-done((bf16[256,2048]{1,0:T(8,128)(2,1)S(1)}, bf16[256,2048]{1,0:T(8,128)(2,1)S(1)}, u32[]{:S(2)}, u32[]{:S(2)}) %collective-permute-start.20) | collective-permute-done | bytes 1048608 | tf_op jit(solution)/shard_map/ppermute | solution.py:267
  400.8 10.3 %collective-permute-done.8 = bf16[256,2048]{1,0:T(8,128)(2,1)S(1)} collective-permute-done((bf16[256,2048]{1,0:T(8,128)(2,1)S(1)}, bf16[256,2048]{1,0:T(8,128)(2,1)S(1)}, u32[]{:S(2)}, u32[]{:S(2)}) %collective-permute-start.8) | collective-permute-done | bytes 1048608 | tf_op jit(solution)/shard_map/ppermute | solution.py:267
  424.9 18.4 %collective-permute-done.35 = f32[13824]{0:T(1024)S(1)} collective-permute-done((f32[13824]{0:T(1024)S(1)}, f32[13824]{0:T(1024)S(1)}, u32[]{:S(2)}, u32[]{:S(2)}) %collective-permute-start.35) | collective-permute-done | bytes 55328 | tf_op jit(solution)/shard_map/ppermute | solution.py:282
  448.2 6.8 add_convert_fusion.1
  457.2 7.9 %add_convert_fusion = bf16[1024,2048]{1,0:T(8,128)(2,1)S(1)} fusion(bf16[1024,2048]{1,0:T(8,128)(2,1)} %collective-permute-done.59, bf16[1024,2048]{1,0:T(8,128)(2,1)} %get-tuple-element.108, s32[]{:T(128)S(6)} %select_n.289, bf16[256,2048]{1,0:T(8,128)(2,1)S(1)} %copy-done.19, bf16[256,2048]{1,0:T(8,128)(2,1)S(1)} %copy-done.16, ...), kind=kOutput, calls=%fused_computation.24 | convolution fusion | flops 4318035968 | bytes 14680068 | tf_op jit(solution)/shard_map/dot_general | solution.py:66
  469.2 29.5 %collective-permute-done.31 = bf16[128,1536]{1,0:T(8,128)(2,1)S(1)} collective-permute-done((bf16[128,1536]{1,0:T(8,128)(2,1)S(1)}, bf16[128,1536]{1,0:T(8,128)(2,1)S(1)}, u32[]{:S(2)}, u32[]{:S(2)}) %collective-permute-start.31) | collective-permute-done | bytes 393248 | tf_op jit(solution)/shard_map/ppermute | solution.py:282
  499.3 9.0 %collective-permute-done.27 = bf16[128,1536]{1,0:T(8,128)(2,1)S(1)} collective-permute-done((bf16[128,1536]{1,0:T(8,128)(2,1)S(1)}, bf16[128,1536]{1,0:T(8,128)(2,1)S(1)}, u32[]{:S(2)}, u32[]{:S(2)}) %collective-permute-start.27) | collective-permute-done | bytes 393248 | tf_op jit(solution)/shard_map/ppermute | solution.py:282
  512.0 22.2 %collective-permute-done.64 = bf16[256,2048]{1,0:T(8,128)(2,1)S(1)} collective-permute-done((bf16[256,2048]{1,0:T(8,128)(2,1)S(1)}, bf16[256,2048]{1,0:T(8,128)(2,1)S(1)}, u32[]{:S(2)}, u32[]{:S(2)}) %collective-permute-start.64) | collective-permute-done | bytes 1048608 | tf_op jit(solution)/shard_map/ppermute | solution.py:282
  537.4 11.1 %collective-permute-done.32 = bf16[256,1536]{1,0:T(8,128)(2,1)S(1)} collective-permute-done((bf16[256,1536]{1,0:T(8,128)(2,1)S(1)}, bf16[256,1536]{1,0:T(8,128)(2,1)S(1)}, u32[]{:S(2)}, u32[]{:S(2)}) %collective-permute-start.32) | collective-permute-done | bytes 786464 | tf_op jit(solution)/shard_map/ppermute | solution.py:282
  555.8 9.4 %collective-permute-done.55 = bf16[128,2048]{1,0:T(8,128)(2,1)S(1)} collective-permute-done((bf16[128,2048]{1,0:T(8,128)(2,1)S(1)}, bf16[128,2048]{1,0:T(8,128)(2,1)S(1)}, u32[]{:S(2)}, u32[]{:S(2)}) %collective-permute-start.55) | collective-permute-done | bytes 524320 | tf_op jit(solution)/shard_map/ppermute | solution.py:282
  584.4 7.8 %collective-permute-done.52 = bf16[128,2048]{1,0:T(8,128)(2,1)S(1)} collective-permute-done((bf16[128,2048]{1,0:T(8,128)(2,1)S(1)}, bf16[128,2048]{1,0:T(8,128)(2,1)S(1)}, u32[]{:S(2)}, u32[]{:S(2)}) %collective-permute-start.52) | collective-permute-done | bytes 524320 | tf_op jit(solution)/shard_map/ppermute | solution.py:282
  595.3 11.9 %collective-permute-done.62 = bf16[128,2048]{1,0:T(8,128)(2,1)S(1)} collective-permute-done((bf16[128,2048]{1,0:T(8,128)(2,1)S(1)}, bf16[128,2048]{1,0:T(8,128)(2,1)S(1)}, u32[]{:S(2)}, u32[]{:S(2)}) %collective-permute-start.62) | collective-permute-done | bytes 524320 | tf_op jit(solution)/shard_map/ppermute | solution.py:282
  607.5 19.5 %collective-permute-done.57 = bf16[256,2048]{1,0:T(8,128)(2,1)S(1)} collective-permute-done((bf16[256,2048]{1,0:T(8,128)(2,1)S(1)}, bf16[256,2048]{1,0:T(8,128)(2,1)S(1)}, u32[]{:S(2)}, u32[]{:S(2)}) %collective-permute-start.57) | collective-permute-done | bytes 1048608 | tf_op jit(solution)/shard_map/ppermute | solution.py:282
  634.8 8.9 %collective-permute-done.67 = bf16[256,2048]{1,0:T(8,128)(2,1)S(1)} collective-permute-done((bf16[256,2048]{1,0:T(8,128)(2,1)S(1)}, bf16[256,2048]{1,0:T(8,128)(2,1)S(1)}, u32[]{:S(2)}, u32[]{:S(2)}) %collective-permute-start.67) | collective-permute-done | bytes 1048608 | tf_op jit(solution)/shard_map/ppermute | solution.py:282
  655.6 6.6 maximum_convert_fusion.2
  668.4 11.8 %maximum_convert_fusion = f32[2048,2048]{1,0:T(8,128)} fusion(bf16[1024,2048]{1,0:T(8,128)(2,1)} %get-tuple-element.35, bf16[1024,2048]{1,0:T(8,128)(2,1)} %get-tuple-element.34), kind=kLoop, calls=%fused_computation.22 | loop fusion | flops 16777216 | bytes 25165824 | tf_op jit(solution)/shard_map/convert_element_type | solution.py:320
  680.3 6.5 broadcast_select_fusion.1
  686.8 12.0 %maximum_convert_fusion.1 = f32[2048,2048]{1,0:T(8,128)} fusion(bf16[1024,2048]{1,0:T(8,128)(2,1)} %get-tuple-element.33, bf16[1024,2048]{1,0:T(8,128)(2,1)} %get-tuple-element.32), kind=kLoop, calls=%fused_computation.23 | loop fusion | flops 16777216 | bytes 25165824 | tf_op jit(solution)/shard_map/convert_element_type | solution.py:320
  (349 shorter events, 260.3 us)
Async XLA Ops:
  0.7 27.8 %collective-permute-start = (bf16[256,2048]{1,0:T(8,128)(2,1)}, bf16[256,2048]{1,0:T(8,128)(2,1)S(1)}, u32[]{:S(2)}, u32[]{:S(2)}) collective-permute-start(bf16[256,2048]{1,0:T(8,128)(2,1)} %param.15), channel_id=1, source_target_pairs={{0,1},{1,2},{2,3},{4,5},{5,6},{6,7},{8,9},{9,10},{10,11},{12,13},{... | collective-permute-start | bytes 3145736 | tf_op jit(solution)/shard_map/ppermute | solution.py:247
  5.8 26.7 %collective-permute-start.1 = (bf16[256,2048]{1,0:T(8,128)(2,1)}, bf16[256,2048]{1,0:T(8,128)(2,1)S(1)}, u32[]{:S(2)}, u32[]{:S(2)}) collective-permute-start(bf16[256,2048]{1,0:T(8,128)(2,1)} %param.15), channel_id=1, source_target_pairs={{1,0},{2,1},{3,2},{5,4},{6,5},{7,6},{9,8},{10,9},{11,10},{13,12},{... | collective-permute-start | bytes 3145736 | tf_op jit(solution)/shard_map/ppermute | solution.py:250
  32.6 27.7 %collective-permute-start.2 = (bf16[256,2048]{1,0:T(8,128)(2,1)S(1)}, bf16[256,2048]{1,0:T(8,128)(2,1)}, u32[]{:S(2)}, u32[]{:S(2)}) collective-permute-start(bf16[256,2048]{1,0:T(8,128)(2,1)S(1)} %collective-permute-done.1), channel_id=1, source_target_pairs={{1,0},{2,1},{5,4},{6,5},{9,8},{10,9},{13,12},{14,13},{17,16},{18,1... | collective-permute-start | bytes 3145736 | tf_op jit(solution)/shard_map/ppermute | solution.py:250
  33.9 40.9 %collective-permute-start.5 = (bf16[256,2048]{1,0:T(8,128)(2,1)}, bf16[256,2048]{1,0:T(8,128)(2,1)}, u32[]{:S(2)}, u32[]{:S(2)}) collective-permute-start(bf16[256,2048]{1,0:T(8,128)(2,1)} %collective-permute-done.4), channel_id=1, source_target_pairs={{2,3},{6,7},{10,11},{14,15},{18,19},{22,23},{26,27},{30,31}} | collective-permute-start | bytes 3145736 | tf_op jit(solution)/shard_map/ppermute | solution.py:247
  60.3 25.4 %collective-permute-start.3 = (bf16[256,2048]{1,0:T(8,128)(2,1)}, bf16[256,2048]{1,0:T(8,128)(2,1)}, u32[]{:S(2)}, u32[]{:S(2)}) collective-permute-start(bf16[256,2048]{1,0:T(8,128)(2,1)} %collective-permute-done.2), channel_id=1, source_target_pairs={{1,0},{5,4},{9,8},{13,12},{17,16},{21,20},{25,24},{29,28}} | collective-permute-start | bytes 3145736 | tf_op jit(solution)/shard_map/ppermute | solution.py:250
  88.1 71.4 %collective-permute-start.12 = (bf16[256,2048]{1,0:T(8,128)(2,1)}, bf16[256,2048]{1,0:T(8,128)(2,1)}, u32[]{:S(2)}, u32[]{:S(2)}) collective-permute-start(bf16[256,2048]{1,0:T(8,128)(2,1)} %param.29), channel_id=1, source_target_pairs={{0,1},{1,2},{2,3},{4,5},{5,6},{6,7},{8,9},{9,10},{10,11},{12,13},{... | collective-permute-start | bytes 3145736 | tf_op jit(solution)/shard_map/ppermute | solution.py:247
  90.9 70.2 %collective-permute-start.13 = (bf16[256,2048]{1,0:T(8,128)(2,1)}, bf16[256,2048]{1,0:T(8,128)(2,1)}, u32[]{:S(2)}, u32[]{:S(2)}) collective-permute-start(bf16[256,2048]{1,0:T(8,128)(2,1)} %param.29), channel_id=1, source_target_pairs={{1,0},{2,1},{3,2},{5,4},{6,5},{7,6},{9,8},{10,9},{11,10},{13,12},{... | collective-permute-start | bytes 3145736 | tf_op jit(solution)/shard_map/ppermute | solution.py:250
  159.5 28.0 %collective-permute-start.16 = (bf16[256,2048]{1,0:T(8,128)(2,1)}, bf16[256,2048]{1,0:T(8,128)(2,1)}, u32[]{:S(2)}, u32[]{:S(2)}) collective-permute-start(bf16[256,2048]{1,0:T(8,128)(2,1)} %collective-permute-done.12), channel_id=1, source_target_pairs={{1,2},{2,3},{5,6},{6,7},{9,10},{10,11},{13,14},{14,15},{17,18},{18... | collective-permute-start | bytes 3145736 | tf_op jit(solution)/shard_map/ppermute | solution.py:247
  161.2 28.0 %collective-permute-start.14 = (bf16[256,2048]{1,0:T(8,128)(2,1)}, bf16[256,2048]{1,0:T(8,128)(2,1)}, u32[]{:S(2)}, u32[]{:S(2)}) collective-permute-start(bf16[256,2048]{1,0:T(8,128)(2,1)} %collective-permute-done.13), channel_id=1, source_target_pairs={{1,0},{2,1},{5,4},{6,5},{9,8},{10,9},{13,12},{14,13},{17,16},{18,1... | collective-permute-start | bytes 3145736 | tf_op jit(solution)/shard_map/ppermute | solution.py:250
  187.5 29.7 %collective-permute-start.17 = (bf16[256,2048]{1,0:T(8,128)(2,1)}, bf16[256,2048]{1,0:T(8,128)(2,1)}, u32[]{:S(2)}, u32[]{:S(2)}) collective-permute-start(bf16[256,2048]{1,0:T(8,128)(2,1)} %collective-permute-done.16), channel_id=1, source_target_pairs={{2,3},{6,7},{10,11},{14,15},{18,19},{22,23},{26,27},{30,31}} | collective-permute-start | bytes 3145736 | tf_op jit(solution)/shard_map/ppermute | solution.py:247
  189.1 30.4 %collective-permute-start.15 = (bf16[256,2048]{1,0:T(8,128)(2,1)}, bf16[256,2048]{1,0:T(8,128)(2,1)}, u32[]{:S(2)}, u32[]{:S(2)}) collective-permute-start(bf16[256,2048]{1,0:T(8,128)(2,1)} %collective-permute-done.14), channel_id=1, source_target_pairs={{1,0},{5,4},{9,8},{13,12},{17,16},{21,20},{25,24},{29,28}} | collective-permute-start | bytes 3145736 | tf_op jit(solution)/shard_map/ppermute | solution.py:250
  209.5 191.3 %collective-permute-start.11 = (bf16[256,2048]{1,0:T(8,128)(2,1)}, bf16[256,2048]{1,0:T(8,128)(2,1)}, u32[]{:S(2)}, u32[]{:S(2)}) collective-permute-start(bf16[256,2048]{1,0:T(8,128)(2,1)} %get-tuple-element.54), channel_id=1, source_target_pairs={{0,1},{1,2},{2,3},{4,5},{5,6},{6,7},{8,9},{9,10},{10,11},{12,13},{... | collective-permute-start | bytes 3145736 | tf_op jit(solution)/shard_map/ppermute | solution.py:270
  313.7 102.3 %collective-permute-start.24 = (bf16[1024,1536]{1,0:T(8,128)(2,1)}, bf16[1024,1536]{1,0:T(8,128)(2,1)}, u32[]{:S(2)}, u32[]{:S(2)}) collective-permute-start(bf16[1024,1536]{1,0:T(8,128)(2,1)} %convolution_convert_fusion), channel_id=1, source_target_pairs={{0,4},{4,0},{8,12},{12,8},{16,20},{20,16},{24,28},{28,24},{1,5},{5... | collective-permute-start | bytes 9437192 | tf_op jit(solution)/shard_map/ppermute | solution.py:282
  331.7 35.0 %collective-permute-start.19 = (bf16[256,2048]{1,0:T(8,128)(2,1)S(1)}, bf16[256,2048]{1,0:T(8,128)(2,1)S(1)}, u32[]{:S(2)}, u32[]{:S(2)}) collective-permute-start(bf16[256,2048]{1,0:T(8,128)(2,1)S(1)} %get-tuple-element.49), channel_id=1, source_target_pairs={{2,1},{3,2},{6,5},{7,6},{10,9},{11,10},{14,13},{15,14},{18,17},{19... | collective-permute-start | bytes 3145736 | tf_op jit(solution)/shard_map/ppermute | solution.py:267
  332.4 34.3 %collective-permute-start.22 = (bf16[256,2048]{1,0:T(8,128)(2,1)S(1)}, bf16[256,2048]{1,0:T(8,128)(2,1)S(1)}, u32[]{:S(2)}, u32[]{:S(2)}) collective-permute-start(bf16[256,2048]{1,0:T(8,128)(2,1)S(1)} %get-tuple-element.50), channel_id=1, source_target_pairs={{0,1},{1,2},{4,5},{5,6},{8,9},{9,10},{12,13},{13,14},{16,17},{17,1... | collective-permute-start | bytes 3145736 | tf_op jit(solution)/shard_map/ppermute | solution.py:270
  372.9 27.0 %collective-permute-start.20 = (bf16[256,2048]{1,0:T(8,128)(2,1)S(1)}, bf16[256,2048]{1,0:T(8,128)(2,1)S(1)}, u32[]{:S(2)}, u32[]{:S(2)}) collective-permute-start(bf16[256,2048]{1,0:T(8,128)(2,1)S(1)} %get-tuple-element.47), channel_id=1, source_target_pairs={{1,0},{2,1},{3,2},{5,4},{6,5},{7,6},{9,8},{10,9},{11,10},{13,12},{... | collective-permute-start | bytes 3145736 | tf_op jit(solution)/shard_map/ppermute | solution.py:267
  380.7 30.5 %collective-permute-start.8 = (bf16[256,2048]{1,0:T(8,128)(2,1)S(1)}, bf16[256,2048]{1,0:T(8,128)(2,1)S(1)}, u32[]{:S(2)}, u32[]{:S(2)}) collective-permute-start(bf16[256,2048]{1,0:T(8,128)(2,1)S(1)} %copy-done.27), channel_id=1, source_target_pairs={{1,0},{2,1},{3,2},{5,4},{6,5},{7,6},{9,8},{10,9},{11,10},{13,12},{... | collective-permute-start | bytes 3145736 | tf_op jit(solution)/shard_map/ppermute | solution.py:267
  385.1 62.6 %collective-permute-start.49 = (bf16[1024,2048]{1,0:T(8,128)(2,1)}, bf16[1024,2048]{1,0:T(8,128)(2,1)}, u32[]{:S(2)}, u32[]{:S(2)}) collective-permute-start(bf16[1024,2048]{1,0:T(8,128)(2,1)} %convolution_convert_fusion.2), channel_id=1, source_target_pairs={{0,4},{4,0},{8,12},{12,8},{16,20},{20,16},{24,28},{28,24},{1,5},{5... | collective-permute-start | bytes 12582920 | tf_op jit(solution)/shard_map/ppermute | solution.py:282
  399.9 55.6 %collective-permute-start.59 = (bf16[1024,2048]{1,0:T(8,128)(2,1)S(1)}, bf16[1024,2048]{1,0:T(8,128)(2,1)}, u32[]{:S(2)}, u32[]{:S(2)}) collective-permute-start(bf16[1024,2048]{1,0:T(8,128)(2,1)S(1)} %copy-done.32), channel_id=1, source_target_pairs={{0,4},{4,0},{8,12},{12,8},{16,20},{20,16},{24,28},{28,24},{1,5},{5... | collective-permute-start | bytes 12582920 | tf_op jit(solution)/shard_map/ppermute | solution.py:282
  443.3 189.4 %collective-permute-start.46 = (bf16[256,2048]{1,0:T(8,128)(2,1)S(1)}, bf16[256,2048]{1,0:T(8,128)(2,1)S(1)}, u32[]{:S(2)}, u32[]{:S(2)}) collective-permute-start(bf16[256,2048]{1,0:T(8,128)(2,1)S(1)} %pad_maximum_fusion.5), channel_id=1, source_target_pairs={{0,4},{4,0},{8,12},{12,8},{16,20},{20,16},{24,28},{28,24},{1,5},{5... | collective-permute-start | bytes 3145736 | tf_op jit(solution)/shard_map/ppermute | solution.py:282
  443.3 189.9 %collective-permute-start.36 = (f32[13824]{0:T(1024)S(1)}, f32[13824]{0:T(1024)}, u32[]{:S(2)}, u32[]{:S(2)}) collective-permute-start(f32[13824]{0:T(1024)S(1)} %add.359), channel_id=1, source_target_pairs={{0,16},{4,20},{8,24},{12,28},{16,0},{20,4},{24,8},{28,12},{1,17},{... | collective-permute-start | bytes 165896 | tf_op jit(solution)/shard_map/ppermute | solution.py:282
  455.6 53.4 %collective-permute-start.54 = (bf16[256,2048]{1,0:T(8,128)(2,1)S(1)}, bf16[256,2048]{1,0:T(8,128)(2,1)S(1)}, u32[]{:S(2)}, u32[]{:S(2)}) collective-permute-start(bf16[256,2048]{1,0:T(8,128)(2,1)S(1)} %constant_dynamic-slice_fusion.4), channel_id=1, source_target_pairs={{0,16},{4,20},{8,24},{12,28},{16,0},{20,4},{24,8},{28,12},{1,17},{... | collective-permute-start | bytes 3145736 | tf_op jit(solution)/shard_map/ppermute | solution.py:282
  465.8 44.3 %collective-permute-start.50 = (bf16[256,2048]{1,0:T(8,128)(2,1)S(1)}, bf16[256,2048]{1,0:T(8,128)(2,1)S(1)}, u32[]{:S(2)}, u32[]{:S(2)}) collective-permute-start(bf16[256,2048]{1,0:T(8,128)(2,1)S(1)} %constant_dynamic-slice_fusion.6), channel_id=1, source_target_pairs={{0,8},{4,12},{8,0},{12,4},{16,24},{20,28},{24,16},{28,20},{1,9},{5... | collective-permute-start | bytes 3145736 | tf_op jit(solution)/shard_map/ppermute | solution.py:282
  466.5 32.2 %collective-permute-start.31 = (bf16[128,1536]{1,0:T(8,128)(2,1)S(1)}, bf16[128,1536]{1,0:T(8,128)(2,1)S(1)}, u32[]{:S(2)}, u32[]{:S(2)}) collective-permute-start(bf16[128,1536]{1,0:T(8,128)(2,1)S(1)} %add_convert_fusion.19), channel_id=1, source_target_pairs={{0,8},{4,12},{8,0},{12,4},{16,24},{20,28},{24,16},{28,20},{1,9},{5... | collective-permute-start | bytes 1179656 | tf_op jit(solution)/shard_map/ppermute | solution.py:282
  508.3 26.0 %collective-permute-start.64 = (bf16[256,2048]{1,0:T(8,128)(2,1)S(1)}, bf16[256,2048]{1,0:T(8,128)(2,1)S(1)}, u32[]{:S(2)}, u32[]{:S(2)}) collective-permute-start(bf16[256,2048]{1,0:T(8,128)(2,1)S(1)} %constant_dynamic-slice_fusion), channel_id=1, source_target_pairs={{0,16},{4,20},{8,24},{12,28},{16,0},{20,4},{24,8},{28,12},{1,17},{... | collective-permute-start | bytes 3145736 | tf_op jit(solution)/shard_map/ppermute | solution.py:282
  509.0 26.3 %collective-permute-start.60 = (bf16[256,2048]{1,0:T(8,128)(2,1)S(1)}, bf16[256,2048]{1,0:T(8,128)(2,1)S(1)}, u32[]{:S(2)}, u32[]{:S(2)}) collective-permute-start(bf16[256,2048]{1,0:T(8,128)(2,1)S(1)} %constant_dynamic-slice_fusion.2), channel_id=1, source_target_pairs={{0,8},{4,12},{8,0},{12,4},{16,24},{20,28},{24,16},{28,20},{1,9},{5... | collective-permute-start | bytes 3145736 | tf_op jit(solution)/shard_map/ppermute | solution.py:282
  510.1 38.4 %collective-permute-start.32 = (bf16[256,1536]{1,0:T(8,128)(2,1)S(1)}, bf16[256,1536]{1,0:T(8,128)(2,1)S(1)}, u32[]{:S(2)}, u32[]{:S(2)}) collective-permute-start(bf16[256,1536]{1,0:T(8,128)(2,1)S(1)} %pad_maximum_fusion.11), channel_id=1, source_target_pairs={{0,16},{4,20},{8,24},{12,28},{16,0},{20,4},{24,8},{28,12},{1,17},{... | collective-permute-start | bytes 2359304 | tf_op jit(solution)/shard_map/ppermute | solution.py:282
  535.3 29.9 %collective-permute-start.55 = (bf16[128,2048]{1,0:T(8,128)(2,1)S(1)}, bf16[128,2048]{1,0:T(8,128)(2,1)S(1)}, u32[]{:S(2)}, u32[]{:S(2)}) collective-permute-start(bf16[128,2048]{1,0:T(8,128)(2,1)S(1)} %constant_dynamic-slice_fusion.3), channel_id=1, source_target_pairs={{0,8},{4,12},{8,0},{12,4},{16,24},{20,28},{24,16},{28,20},{1,9},{5... | collective-permute-start | bytes 1572872 | tf_op jit(solution)/shard_map/ppermute | solution.py:282
  566.6 87.6 %collective-permute-start.33 = (bf16[1024,1536]{1,0:T(8,128)(2,1)S(1)}, bf16[1024,1536]{1,0:T(8,128)(2,1)S(1)}, u32[]{:S(2)}, u32[]{:S(2)}) collective-permute-start(bf16[1024,1536]{1,0:T(8,128)(2,1)S(1)} %pad_maximum_fusion.4), channel_id=1, source_target_pairs={{0,4},{4,0},{8,12},{12,8},{16,20},{20,16},{24,28},{28,24},{1,5},{5... | collective-permute-start | bytes 9437192 | tf_op jit(solution)/shard_map/ppermute | solution.py:282
  594.6 32.5 %collective-permute-start.57 = (bf16[256,2048]{1,0:T(8,128)(2,1)S(1)}, bf16[256,2048]{1,0:T(8,128)(2,1)S(1)}, u32[]{:S(2)}, u32[]{:S(2)}) collective-permute-start(bf16[256,2048]{1,0:T(8,128)(2,1)S(1)} %pad_maximum_fusion.7), channel_id=1, source_target_pairs={{0,16},{4,20},{8,24},{12,28},{16,0},{20,4},{24,8},{28,12},{1,17},{... | collective-permute-start | bytes 3145736 | tf_op jit(solution)/shard_map/ppermute | solution.py:282
  632.7 29.4 %collective-permute-start.58 = (bf16[1024,2048]{1,0:T(8,128)(2,1)}, bf16[1024,2048]{1,0:T(8,128)(2,1)}, u32[]{:S(2)}, u32[]{:S(2)}) collective-permute-start(bf16[1024,2048]{1,0:T(8,128)(2,1)} %pad_maximum_fusion.2), channel_id=1, source_target_pairs={{0,4},{4,0},{8,12},{12,8},{16,20},{20,16},{24,28},{28,24},{1,5},{5... | collective-permute-start | bytes 12582920 | tf_op jit(solution)/shard_map/ppermute | solution.py:282
  647.8 32.5 %collective-permute-start.68 = (bf16[1024,2048]{1,0:T(8,128)(2,1)}, bf16[1024,2048]{1,0:T(8,128)(2,1)}, u32[]{:S(2)}, u32[]{:S(2)}) collective-permute-start(bf16[1024,2048]{1,0:T(8,128)(2,1)} %pad_maximum_fusion.3), channel_id=1, source_target_pairs={{0,4},{4,0},{8,12},{12,8},{16,20},{20,16},{24,28},{28,24},{1,5},{5... | collective-permute-start | bytes 12582920 | tf_op jit(solution)/shard_map/ppermute | solution.py:282
  (80 other events, 1230.6 us)

commit v2 on v1

v2 whole, which is shorter than its diff:
```python
import jax
import jax.numpy as jnp
from jax import lax
from jax.experimental import pallas as pl
from jax.experimental.pallas import tpu as pltpu
from jax.sharding import PartitionSpec as P

HEAD_DIM = 128
ROT = 32
EPSILON = 1e-05
MASKED = -1e30
BF16 = jnp.bfloat16
F32 = jnp.float32


def standardize(row_block):
    average = jnp.mean(row_block, axis=1, keepdims=True)
    centred = row_block - average
    inverse = lax.rsqrt(jnp.mean(centred * centred, axis=1, keepdims=True) + EPSILON)
    return (centred * inverse, inverse)


def layout(lengths, group_size):
    seq_ends = jnp.cumsum(lengths)
    row_ids = jnp.arange(group_size, dtype=jnp.int32)
    passed = (seq_ends[None, :] <= row_ids[:, None]).astype(jnp.int32)
    first_row = jnp.sum(passed * lengths[None, :], axis=1)
    return (first_row, row_ids - first_row)


def rotary_tables(position):
    exponents = jnp.arange(0, ROT, 2, dtype=F32) / ROT
    inv_freq = 1.0 / 10000.0**exponents
    angles = position.astype(F32)[:, None] * inv_freq[None, :]
    cosine, sine = jnp.cos(angles), jnp.sin(angles)
    rows, half = angles.shape
    keep = jnp.concatenate([cosine, cosine, jnp.ones((rows, HEAD_DIM - ROT), F32)], axis=1)
    low = jnp.concatenate([-sine, jnp.zeros((rows, HEAD_DIM - half), F32)], axis=1)
    high = jnp.concatenate(
        [jnp.zeros((rows, half), F32), sine, jnp.zeros((rows, HEAD_DIM - ROT), F32)], axis=1
    )
    return (keep, low, high)


def turn(u, keep, low, high):
    return (
        u * keep
        + pltpu.roll(u, HEAD_DIM - ROT // 2, 1) * low
        + pltpu.roll(u, ROT // 2, 1) * high
    )


def turn_back(u, keep, low, high):
    return (
        u * keep
        - pltpu.roll(u, HEAD_DIM - ROT // 2, 1) * low
        - pltpu.roll(u, ROT // 2, 1) * high
    )


def dot_nt(a, b):
    return lax.dot_general(a, b, (((1,), (1,)), ((), ())), preferred_element_type=F32)


def dot_tn(a, b):
    return lax.dot_general(a, b, (((0,), (0,)), ((), ())), preferred_element_type=F32)


def dot_nn(a, b):
    return jnp.dot(a, b, preferred_element_type=F32)


def attend_kernel(blocks, mixed_ref, keep_ref, low_ref, high_ref, first_ref, qkv_ref, context_ref):
    rows = mixed_ref.shape[0] // blocks
    scale = HEAD_DIM ** (-0.5)

    def slot(i):
        return slice(i * rows, (i + 1) * rows)

    for i in range(blocks):
        here = slice(i * rows, (i + 1) * rows)
        tables = (keep_ref[here, :], low_ref[here, :], high_ref[here, :])
        there = slot(i)
        qkv_ref[here, 0:128] = turn(mixed_ref[there, 0:128], *tables).astype(BF16)
        qkv_ref[here, 128:256] = turn(mixed_ref[there, 128:256], *tables).astype(BF16)
        qkv_ref[here, 256:384] = mixed_ref[there, 256:384].astype(BF16)
    for i in range(blocks):
        count = (i + 1) * rows
        query = qkv_ref[i * rows : count, 0:128]
        scores = dot_nt(query, qkv_ref[0:count, 128:256]) * scale
        key_at = lax.broadcasted_iota(jnp.int32, scores.shape, 1)
        query_at = lax.broadcasted_iota(jnp.int32, scores.shape, 0) + i * rows
        seen = (key_at >= first_ref[i * rows : count, :]) & (key_at <= query_at)
        scores = jnp.where(seen, scores, MASKED)
        top = jnp.max(scores, axis=1, keepdims=True)
        raised = jnp.exp(scores - top)
        total = jnp.sum(raised, axis=1, keepdims=True)
        weights = (raised * (1.0 / total)).astype(BF16)
        context_ref[slot(i), :] = dot_nn(weights, qkv_ref[0:count, 256:384]).astype(BF16)


def attend(mixed, tables, first_row, blocks):
    group, width = mixed.shape
    heads = width // (3 * HEAD_DIM)
    whole = lambda h: (0, 0)
    by_head = lambda h: (0, h)
    table = pl.BlockSpec((group, HEAD_DIM), whole)
    return pl.pallas_call(
        lambda *refs: attend_kernel(blocks, *refs),
        out_shape=(
            jax.ShapeDtypeStruct((group, width), BF16),
            jax.ShapeDtypeStruct((group, heads * HEAD_DIM), BF16),
        ),
        grid_spec=pltpu.PrefetchScalarGridSpec(
            num_scalar_prefetch=0,
            grid=(heads,),
            in_specs=[
                pl.BlockSpec((group, 3 * HEAD_DIM), by_head),
                table,
                table,
                table,
                pl.BlockSpec((group, 1), whole),
            ],
            out_specs=(
                pl.BlockSpec((group, 3 * HEAD_DIM), by_head),
                pl.BlockSpec((group, HEAD_DIM), by_head),
            ),
        ),
        compiler_params=pltpu.CompilerParams(dimension_semantics=("arbitrary",)),
        name="attend",
    )(mixed, *tables, first_row[:, None])


def attend_back_kernel(
    blocks,
    qkv_ref,
    grad_ref,
    keep_ref,
    low_ref,
    high_ref,
    first_ref,
    mixed_ref,
    sums_ref,
    keys_ref,
    values_ref,
):
    rows = qkv_ref.shape[0] // blocks
    scale = HEAD_DIM ** (-0.5)

    def slot(i):
        return slice(i * rows, (i + 1) * rows)

    def tables(i):
        here = slice(i * rows, (i + 1) * rows)
        return (keep_ref[here, :], low_ref[here, :], high_ref[here, :])

    query_sum = jnp.zeros((1, HEAD_DIM), F32)
    key_sum = jnp.zeros((1, HEAD_DIM), F32)
    value_sum = jnp.zeros((1, HEAD_DIM), F32)
    for i in reversed(range(blocks)):
        count = (i + 1) * rows
        query = qkv_ref[i * rows : count, 0:128]
        keys = qkv_ref[0:count, 128:256]
        grad = grad_ref[slot(i), :]
        scores = dot_nt(keys, query) * scale
        key_at = lax.broadcasted_iota(jnp.int32, scores.shape, 0)
        query_at = lax.broadcasted_iota(jnp.int32, scores.shape, 1) + i * rows
        seen = (key_at >= first_ref[:, i * rows : count]) & (key_at <= query_at)
        scores = jnp.where(seen, scores, MASKED)
        top = jnp.max(scores, axis=0, keepdims=True)
        raised = jnp.exp(scores - top)
        total = jnp.sum(raised, axis=0, keepdims=True)
        probs = raised * (1.0 / total)
        grad_values = dot_nn(probs.astype(BF16), grad)
        grad_probs = dot_nt(qkv_ref[0:count, 256:384], grad)
        spread = jnp.sum(probs * grad_probs, axis=0, keepdims=True)
        grad_scores = (probs * (grad_probs - spread)).astype(BF16)
        grad_keys = dot_nn(grad_scores, query)
        if i == blocks - 1:
            values_ref[...] = grad_values
            keys_ref[...] = grad_keys
        else:
            values_ref[0:count, :] += grad_values
            keys_ref[0:count, :] += grad_keys
        grad_query = turn_back(dot_tn(grad_scores, keys) * scale, *tables(i)).astype(BF16)
        mixed_ref[slot(i), 0:128] = grad_query
        query_sum += jnp.sum(grad_query.astype(F32), axis=0, keepdims=True)
        here = slice(i * rows, count)
        if i == 0:
            for j in range(blocks):
                here = slice(j * rows, (j + 1) * rows)
                grad_key = turn_back(keys_ref[here, :] * scale, *tables(j)).astype(BF16)
                grad_value = values_ref[here, :].astype(BF16)
                mixed_ref[slot(j), 128:256] = grad_key
                mixed_ref[slot(j), 256:384] = grad_value
                key_sum += jnp.sum(grad_key.astype(F32), axis=0, keepdims=True)
                value_sum += jnp.sum(grad_value.astype(F32), axis=0, keepdims=True)
    sums_ref[:, 0:128] = jnp.broadcast_to(query_sum, (8, HEAD_DIM))
    sums_ref[:, 128:256] = jnp.broadcast_to(key_sum, (8, HEAD_DIM))
    sums_ref[:, 256:384] = jnp.broadcast_to(value_sum, (8, HEAD_DIM))


def attend_back(qkv, grad_context, tables, first_row, blocks):
    group, width = qkv.shape
    heads = width // (3 * HEAD_DIM)
    whole = lambda h: (0, 0)
    by_head = lambda h: (0, h)
    table = pl.BlockSpec((group, HEAD_DIM), whole)
    mixed, sums = pl.pallas_call(
        lambda *refs: attend_back_kernel(blocks, *refs),
        out_shape=(
            jax.ShapeDtypeStruct((group, width), BF16),
            jax.ShapeDtypeStruct((8, width), F32),
        ),
        grid_spec=pltpu.PrefetchScalarGridSpec(
            num_scalar_prefetch=0,
            grid=(heads,),
            in_specs=[
                pl.BlockSpec((group, 3 * HEAD_DIM), by_head),
                pl.BlockSpec((group, HEAD_DIM), by_head),
                table,
                table,
                table,
                pl.BlockSpec((1, group), whole),
            ],
            out_specs=(
                pl.BlockSpec((group, 3 * HEAD_DIM), by_head),
                pl.BlockSpec((8, 3 * HEAD_DIM), by_head),
            ),
            scratch_shapes=[pltpu.VMEM((group, HEAD_DIM), F32)] * 2,
        ),
        compiler_params=pltpu.CompilerParams(dimension_semantics=("arbitrary",)),
        name="attend_back",
    )(qkv, grad_context, *tables, first_row[None, :])
    return (mixed, sums[0])


def forward_kernel(
    up_steps,
    rows_ref,
    gain_attn_ref,
    shift_attn_ref,
    gain_mlp_ref,
    shift_mlp_ref,
    up_ref,
    up_bias_ref,
    qkv_ref,
    qkv_bias_ref,
    *refs,
):
    outs = refs[-9:]
    all_ref, attn_ref, mlp_ref, mean_ref, inverse_ref, active_ref, slope_ref, mixed_ref = outs[:8]
    scratch_ref = outs[8]
    devices, _, rows, width = attn_ref.shape
    at = pl.program_id(0)

    @pl.when(at == 0)
    def _():
        for d in range(devices):
            here = slice(d * rows, (d + 1) * rows)
            piece = rows_ref[here, :]
            values = piece.astype(F32)
            average = jnp.mean(values, axis=1, keepdims=True)
            centred = values - average
            inverse = lax.rsqrt(jnp.mean(centred * centred, axis=1, keepdims=True) + EPSILON)
            scaled = centred * inverse
            attn = (scaled * gain_attn_ref[...] + shift_attn_ref[...]).astype(BF16)
            mlp = (scaled * gain_mlp_ref[...] + shift_mlp_ref[...]).astype(BF16)
            all_ref[d, 0] = piece
            attn_ref[d, 0] = attn
            mlp_ref[d, 0] = mlp
            mean_ref[d, 0] = average
            inverse_ref[d, 0] = inverse
            scratch_ref[0, here, :] = mlp
            scratch_ref[1, here, :] = attn

    @pl.when(at < up_steps)
    def _():
        for d in range(devices):
            here = slice(d * rows, (d + 1) * rows)
            hidden = dot_nn(scratch_ref[0, here, :], up_ref[...]) + up_bias_ref[...]
            below = 0.5 * (1.0 + lax.erf(hidden * 0.5**0.5))
            bell = jnp.exp(-0.5 * hidden * hidden) * (2.0 * jnp.pi) ** -0.5
            active_ref[d, 0] = (hidden * below).astype(BF16)
            slope_ref[d, 0] = (below + hidden * bell).astype(BF16)

    @pl.when(at >= up_steps)
    def _():
        for d in range(devices):
            here = slice(d * rows, (d + 1) * rows)
            mixed_ref[d, 0] = dot_nn(scratch_ref[1, here, :], qkv_ref[...]) + qkv_bias_ref[...]


def forward(gathered, part, vectors, up_weight, up_bias, qkv_weight, qkv_bias, devices, buffers):
    count, width = gathered.shape
    rows = count // devices
    hidden, third = up_weight.shape[1], qkv_weight.shape[1]
    up_part, qkv_part = hidden // 4, third // 3
    up_steps, steps = 4, 7
    up_at = lambda j: jnp.minimum(j, up_steps - 1)
    qkv_at = lambda j: jnp.maximum(j - up_steps, 0)
    vector = pl.BlockSpec((1, width), lambda j: (0, 0))
    whole = lambda n: pl.BlockSpec((devices, 1, rows, n), lambda j: (0, part, 0, 0))
    up_out = pl.BlockSpec((devices, 1, rows, up_part), lambda j: (0, part, 0, up_at(j)))
    shape = lambda n, t: jax.ShapeDtypeStruct((devices, 2, rows, n), t)
    return pl.pallas_call(
        lambda *refs: forward_kernel(up_steps, *refs),
        out_shape=[
            shape(width, BF16),
            shape(width, BF16),
            shape(width, BF16),
            shape(1, F32),
            shape(1, F32),
            shape(hidden, BF16),
            shape(hidden, BF16),
            shape(third, F32),
        ],
        grid=(steps,),
        in_specs=[pl.BlockSpec((count, width), lambda j: (0, 0))]
        + [vector] * 4
        + [
            pl.BlockSpec((width, up_part), lambda j: (0, up_at(j))),
            pl.BlockSpec((1, up_part), lambda j: (0, up_at(j))),
            pl.BlockSpec((width, qkv_part), lambda j: (0, qkv_at(j))),
            pl.BlockSpec((1, qkv_part), lambda j: (0, qkv_at(j))),
        ]
        + [pl.BlockSpec(memory_space=pl.ANY)] * len(buffers),
        out_specs=[
            whole(width),
            whole(width),
            whole(width),
            whole(1),
            whole(1),
            up_out,
            up_out,
            pl.BlockSpec((devices, 1, rows, qkv_part), lambda j: (0, part, 0, qkv_at(j))),
        ],
        scratch_shapes=[pltpu.VMEM((2, count, width), BF16)],
        input_output_aliases={9 + k: k for k in range(len(buffers))},
        name="forward",
    )(
        gathered,
        *vectors,
        up_weight,
        up_bias.astype(F32)[None, :],
        qkv_weight,
        qkv_bias.astype(F32)[None, :],
        *buffers,
    )


def hidden_back_kernel(sloped, one_ref, two_ref, weight_ref, *refs):
    group, half = one_ref.shape
    grad_ref = refs[1] if sloped else refs[0]
    step = min(group, 256)
    sums = jnp.zeros((1, grad_ref.shape[1]), F32)
    for r in range(0, group, step):
        here = slice(r, r + step)
        grad = dot_nt(one_ref[here, :], weight_ref[:, :half])
        grad += dot_nt(two_ref[here, :], weight_ref[:, half:])
        if sloped:
            grad = grad * refs[0][here, :].astype(F32)
        grad = grad.astype(BF16)
        grad_ref[here, :] = grad
        if sloped:
            sums += jnp.sum(grad.astype(F32), axis=0, keepdims=True)
    if sloped:
        refs[2][...] = jnp.broadcast_to(sums, refs[2].shape)


def hidden_back(one, two, weight, slope=None):
    group, half = one.shape
    hidden = weight.shape[0]
    sloped = slope is not None
    part = min(hidden, 512 if sloped else 256)
    kept = pl.BlockSpec((group, half), lambda j: (0, 0), pipeline_mode=pl.Buffered(1))
    columns = pl.BlockSpec((group, part), lambda j: (0, j))
    out = [jax.ShapeDtypeStruct((group, hidden), BF16), jax.ShapeDtypeStruct((8, hidden), F32)]
    specs = [columns, pl.BlockSpec((8, part), lambda j: (0, j))]
    count = 2 if sloped else 1
    return pl.pallas_call(
        lambda *refs: hidden_back_kernel(sloped, *refs),
        out_shape=out[:count],
        grid=(hidden // part,),
        in_specs=[kept, kept, pl.BlockSpec((part, 2 * half), lambda j: (j, 0))]
        + ([columns] if sloped else []),
        out_specs=specs[:count],
        name="hidden_back" if sloped else "context_back",
    )(one, two, weight, *((slope,) if sloped else ()))


def inner_kernel(
    hidden_ref,
    up_ref,
    mixed_ref,
    qkv_ref,
    rows_ref,
    mean_ref,
    inverse_ref,
    gain_attn_ref,
    gain_mlp_ref,
    inner_ref,
    sums_ref,
):
    group, width = inner_ref.shape
    step = min(group, 256)
    totals = [jnp.zeros((1, width), F32) for _ in range(4)]
    for r in range(0, group, step):
        here = slice(r, r + step)
        mlp = dot_nt(hidden_ref[here, :], up_ref[...])
        attn = dot_nt(mixed_ref[here, :], qkv_ref[...])
        scaled = (rows_ref[here, :].astype(F32) - mean_ref[here, :]) * inverse_ref[here, :]
        inner_ref[here, :] = (mlp * gain_mlp_ref[...] + attn * gain_attn_ref[...]).astype(BF16)
        for k, term in enumerate((attn * scaled, attn, mlp * scaled, mlp)):
            totals[k] += jnp.sum(term, axis=0, keepdims=True)
    for k in range(4):
        sums_ref[k : k + 1, :] = totals[k]


def inner_grad(grad_hidden, up_weight, grad_mixed, qkv_weight, rows, mean, inverse, gains):
    group, hidden = grad_hidden.shape
    third = grad_mixed.shape[1]
    width = rows.shape[1]
    part = min(width, 512)
    once = pl.Buffered(1)
    row = pl.BlockSpec((1, part), lambda j: (0, j))
    columns = pl.BlockSpec((group, part), lambda j: (0, j))
    column = pl.BlockSpec((group, 1), lambda j: (0, 0))
    return pl.pallas_call(
        inner_kernel,
        out_shape=(
            jax.ShapeDtypeStruct((group, width), BF16),
            jax.ShapeDtypeStruct((4, width), F32),
        ),
        grid=(width // part,),
        in_specs=[
            pl.BlockSpec((group, hidden), lambda j: (0, 0), pipeline_mode=once),
            pl.BlockSpec((part, hidden), lambda j: (j, 0)),
            pl.BlockSpec((group, third), lambda j: (0, 0), pipeline_mode=once),
            pl.BlockSpec((part, third), lambda j: (j, 0)),
            columns,
            column,
            column,
            row,
            row,
        ],
        out_specs=(columns, pl.BlockSpec((4, part), lambda j: (0, j))),
        name="inner_grad",
    )(grad_hidden, up_weight, grad_mixed, qkv_weight, rows, mean, inverse, *gains)


def widen_kernel(rows, offset, column, sides_ref, *refs):
    pieces, out_ref = refs[:8], refs[-5]
    came, wide, came_sems, wide_sems = refs[-4:]
    width = wide.shape[2]

    def bring(k):
        source = pieces[k].at[offset : offset + rows, :]
        return pltpu.make_async_copy(source, came.at[k], came_sems.at[k])

    def send(k):
        at = (((k >> 2) ^ sides_ref[0]) << 2) + (k & 2) + ((k & 1) ^ sides_ref[1 + ((k >> 1) & 1)])
        target = out_ref.at[
            pl.ds(pl.multiple_of(at * rows, rows), rows), column * width : (column + 1) * width
        ]
        return pltpu.make_async_copy(wide.at[k & 1], target, wide_sems.at[k])

    for k in range(8):
        bring(k).start()
    for k in range(8):
        bring(k).wait()
        if k > 1:
            send(k - 2).wait()
        wide[k & 1] = came[k].astype(F32)
        send(k).start()
    send(6).wait()
    send(7).wait()


def widen(pieces, sides, rows, offset, full, column, buffers):
    width = pieces[0].shape[1]
    anywhere = pl.BlockSpec(memory_space=pl.ANY)
    return pl.pallas_call(
        lambda *refs: widen_kernel(rows, offset, column, *refs),
        out_shape=jax.ShapeDtypeStruct(full, F32),
        grid_spec=pltpu.PrefetchScalarGridSpec(
            num_scalar_prefetch=1,
            grid=(),
            in_specs=[anywhere] * (8 + len(buffers)),
            out_specs=anywhere,
            scratch_shapes=[
                pltpu.VMEM((8, rows, width), BF16),
                pltpu.VMEM((2, rows, width), F32),
                pltpu.SemaphoreType.DMA((8,)),
                pltpu.SemaphoreType.DMA((8,)),
            ],
        ),
        input_output_aliases={9: 0} if buffers else {},
        name="widen",
    )(sides, *pieces, *buffers)


def after(value, *earlier):
    return lax.optimization_barrier((value, *earlier))[0]


class Order:
    def __init__(self):
        self.last = ()

    def __call__(self, work, *inputs):
        inputs, _ = lax.optimization_barrier((inputs, self.last))
        result = work(*inputs)
        self.last = result
        return result

    def wait(self, *values):
        self.last = (self.last, values)


class Groups:
    def __init__(self):
        self.size = lax.axis_size("dp")
        self.bits = self.size.bit_length() - 1
        me = lax.axis_index("dp")
        self.side = [(me >> b) & 1 for b in range(self.bits)]
        self.order_a = list(range(1, self.bits))
        self.order_b = self.order_a[1:] + self.order_a[:1]
        self.sides = jnp.stack(
            [self.side[0], self.side[self.order_a[0]], self.side[self.order_b[0]]]
        ).astype(jnp.int32)

    def swap(self, value, bit):
        return lax.ppermute(value, "dp", [(i, i ^ (1 << bit)) for i in range(self.size)])

    def half(self, value, bit, own, axis=0):
        half = value.shape[axis] // 2
        side = self.side[bit] if own else 1 - self.side[bit]
        return lax.dynamic_slice_in_dim(value, side * half, half, axis)

    def join(self, mine, theirs, bit):
        first = self.side[bit] == 0
        return jnp.concatenate(
            [jnp.where(first, mine, theirs), jnp.where(first, theirs, mine)], axis=0
        )

    def chunk(self, run, lefts, right):
        sizes = [left.shape[1] for left in lefts]

        def product(own, *came):
            def work(right, *values):
                out = []
                for k in range(len(lefts)):
                    value = dot_tn(self.half(values[k], 0, own, 1), right)
                    if own:
                        value = value + values[len(lefts) + k].astype(F32)
                    out.append(value.astype(BF16))
                return tuple(out)

            return run(work, right, *lefts, *came)

        came = tuple(self.swap(value, 0) for value in product(False))
        yield None
        both = product(True, *came)

        def split(both):
            branch = lambda b: [
                p[: p.shape[0] // 2] if b == 0 else p[p.shape[0] // 2 :] for p in both
            ]
            return [branch(0), branch(1)]

        def rows_of(parts):
            return parts[0] if len(parts) == 1 else jnp.concatenate(parts, axis=0)

        def cut(value, like):
            out, start = [], 0
            for n in like:
                out.append(value[start : start + n])
                start += n
            return out

        orders = (self.order_a, self.order_b)
        counts = [n // 4 for n in sizes]

        def first_gives(*both):
            branches = split(both)
            return tuple(
                rows_of([self.half(p, orders[b][0], False) for p in branches[b]]) for b in (0, 1)
            )

        def first_keeps(*both):
            branches = split(both)
            return tuple(
                rows_of([self.half(p, orders[b][0], True) for p in branches[b]]) for b in (0, 1)
            )

        gives = run(first_gives, *both)
        keeps = None
        for step in range(self.bits - 1):
            got = tuple(self.swap(gives[b], orders[b][step]) for b in (0, 1))
            yield None
            counts = [n // 2 for n in counts]
            first, last = step == 0, step == self.bits - 2

            def add(*values):
                *kept, got_a, got_b = values
                kept = first_keeps(*kept) if first else kept
                sums = [
                    (k.astype(F32) + g.astype(F32)).astype(BF16)
                    for k, g in zip(kept, (got_a, got_b))
                ]
                if last:
                    return tuple(sums)
                parts = [cut(s, counts) for s in sums]
                pick = lambda own: tuple(
                    rows_of([self.half(p, orders[b][step + 1], own) for p in parts[b]])
                    for b in (0, 1)
                )
                return pick(False) + pick(True)

            out = run(add, *(both if first else keeps), *got)
            gives, keeps = out[:2], out[2:]
        done = gives
        for step in reversed(range(1, self.bits - 1)):
            got = tuple(self.swap(done[b], orders[b][step]) for b in (0, 1))
            yield None

            def joins(*values):
                out = []
                for b in (0, 1):
                    mine, theirs = cut(values[b], counts), cut(values[2 + b], counts)
                    out.append(
                        rows_of(
                            [self.join(m, t, orders[b][step]) for m, t in zip(mine, theirs)]
                        )
                    )
                return tuple(out)

            done = run(joins, *done, *got)
            counts = [n * 2 for n in counts]
        got = tuple(self.swap(done[b], orders[b][0]) for b in (0, 1))
        near = tuple(self.swap(done[b], 0) for b in (0, 1))
        yield None
        run.wait(*got)
        far = tuple(self.swap(got[b], 0) for b in (0, 1))
        yield ((done[0], got[0], done[1], got[1], near[0], far[0], near[1], far[1]), counts)


def small_sum(run, groups, shared, split, size):
    add = lambda a, b: a + b
    for bit in range(groups.bits):
        got = groups.swap(shared, bit)
        yield None
        shared = run(add, shared, got)
    everywhere = shared[:, :split]
    reach = 1
    while reach < size:
        got = lax.ppermute(everywhere, "tensor", [(i, i ^ reach) for i in range(size)])
        yield None
        everywhere = run(add, everywhere, got)
        reach *= 2
    yield everywhere[0], shared[0, split:]


def shards(
    tokens,
    lengths,
    qkv_weight,
    qkv_bias,
    dense_weight,
    dense_bias,
    up_weight,
    up_bias,
    down_weight,
    down_bias,
    gain_attn,
    shift_attn,
    gain_mlp,
    shift_mlp,
    out_grad,
):
    size = lax.axis_size("tensor")
    width = tokens.shape[1]
    own_rows = tokens.shape[0]
    group_size = own_rows * size
    blocks = max(group_size // 256, 1)
    groups = Groups()
    run = Order()
    half = width // 2

    top = lax.all_gather(tokens[: own_rows // 2], "tensor", axis=0, tiled=True)
    bottom = lax.all_gather(after(tokens[own_rows // 2 :], top), "tensor", axis=0, tiled=True)
    grad_one = lax.all_gather(after(out_grad[:, :half], bottom), "tensor", axis=0, tiled=True)
    grad_two = lax.all_gather(after(out_grad[:, half:], grad_one), "tensor", axis=0, tiled=True)

    first_row, position = layout(lengths[0], group_size)
    tables = rotary_tables(position)
    vectors = [v.astype(F32)[None, :] for v in (gain_attn, shift_attn, gain_mlp, shift_mlp)]
    tokens_own = tokens.astype(F32)
    grad_rows = out_grad.astype(F32)
    bias_part = jnp.sum(grad_rows, axis=0)

    buffers = ()
    for part, gathered in enumerate((top, bottom)):
        buffers = run(
            lambda g, *b: forward(
                g, part, vectors, up_weight, up_bias, qkv_weight, qkv_bias, size, b
            ),
            gathered,
            *buffers,
        )
    rows, normed_attn, normed_mlp, mean, inverse, active, slope, mixed = (
        b.reshape(group_size, b.shape[3]) for b in buffers
    )
    qkv, context = run(lambda m: attend(m, tables, first_row, blocks), mixed)
    down_one = groups.chunk(run, [active, context], grad_one)
    next(down_one)
    next(down_one)
    partial = run(
        lambda c, a: (dot_nn(c, dense_weight) + dot_nn(a, down_weight)).astype(BF16),
        context,
        active,
    )
    branches = lax.psum_scatter(
        after(partial, grad_two), "tensor", scatter_dimension=0, tiled=True
    )
    next(down_one)
    next(down_one)
    down_two = groups.chunk(run, [active, context], grad_two)
    next(down_two)
    next(down_one)
    next(down_two)
    grad_hidden, up_bias_part = run(
        lambda a, b: hidden_back(a, b, down_weight, slope), grad_one, grad_two
    )
    pieces_one, counts = final(down_one)
    up = groups.chunk(run, [normed_mlp], grad_hidden)
    next(up)
    next(down_two)
    next(up)
    (grad_context,) = run(lambda a, b: hidden_back(a, b, dense_weight), grad_one, grad_two)
    next(down_two)
    grad_mixed, qkv_bias_part = run(
        lambda q, g: attend_back(q, g, tables, first_row, blocks), qkv, grad_context
    )
    next(down_two)
    next(up)
    inner, sums = run(
        lambda h, m: inner_grad(
            h, up_weight, m, qkv_weight, rows, mean, inverse, (vectors[0], vectors[2])
        ),
        grad_hidden,
        grad_mixed,
    )
    inner_own = lax.psum_scatter(inner, "tensor", scatter_dimension=0, tiled=True)
    pieces_two, counts = final(down_two)
    next(up)
    last = groups.chunk(run, [normed_attn], grad_mixed)
    next(last)
    next(last)
    next(up)
    split = 5 * width
    shared = jnp.concatenate([sums.reshape(-1), bias_part, up_bias_part[0], qkv_bias_part])
    totals = small_sum(run, groups, shared[None, :], split, size)
    full_down, full_dense = down_weight.shape, dense_weight.shape
    grad_down = run(
        lambda *p: widen(p, groups.sides, counts[0], 0, full_down, 0, ()), *pieces_one
    )
    next(totals)
    grad_dense = run(
        lambda *p: widen(p, groups.sides, counts[1], counts[0], full_dense, 0, ()), *pieces_one
    )
    next(totals)
    grad_down = run(
        lambda b, *p: widen(p, groups.sides, counts[0], 0, full_down, 1, (b,)),
        grad_down,
        *pieces_two,
    )
    next(last)
    next(totals)
    grad_dense = run(
        lambda b, *p: widen(p, groups.sides, counts[1], counts[0], full_dense, 1, (b,)),
        grad_dense,
        *pieces_two,
    )
    output = run(
        lambda b: (
            tokens.astype(F32) + b.astype(F32) + dense_bias.astype(F32) + down_bias.astype(F32)
        ).astype(BF16),
        branches,
    )
    next(last)
    pieces_up, counts = final(up)
    next(totals)
    next(last)
    grad_up = run(
        lambda *p: widen(p, groups.sides, counts[0], 0, up_weight.shape, 0, ()), *pieces_up
    )
    next(totals)
    everywhere, here = final(totals)

    def tokens_work(inner_own):
        inner_own = inner_own.astype(F32)
        scaled_own, inverse_own = standardize(tokens_own)
        return grad_rows + inverse_own * (
            inner_own
            - jnp.mean(inner_own, axis=1, keepdims=True)
            - scaled_own * jnp.mean(inner_own * scaled_own, axis=1, keepdims=True)
        )

    pieces_last, counts = final(last)
    grad_qkv = run(
        lambda *p: widen(p, groups.sides, counts[0], 0, qkv_weight.shape, 0, ()), *pieces_last
    )
    grad_tokens = run(tokens_work, inner_own)
    gain_attn_sum, shift_attn_sum, gain_mlp_sum, shift_mlp_sum, bias_sum = (
        everywhere[k * width : (k + 1) * width] for k in range(5)
    )
    return (
        output,
        grad_tokens,
        grad_qkv,
        here[up_bias.shape[0] :],
        grad_dense,
        bias_sum,
        grad_up,
        here[: up_bias.shape[0]],
        grad_down,
        bias_sum,
        gain_attn_sum,
        shift_attn_sum,
        gain_mlp_sum,
        shift_mlp_sum,
    )


def final(stages):
    *_, result = stages
    return result


def solution(mesh):
    rows = P(("dp", "tensor"), None)
    columns = P(None, "tensor")
    return jax.shard_map(
        shards,
        mesh=mesh,
        in_specs=(
            rows,
            P("dp", None),
            columns,
            P("tensor"),
            P("tensor", None),
            P(),
            columns,
            P("tensor"),
            P("tensor", None),
            P(),
            P(),
            P(),
            P(),
            P(),
            rows,
        ),
        out_specs=(
            rows,
            rows,
            columns,
            P("tensor"),
            P("tensor", None),
            P(),
            columns,
            P("tensor"),
            P("tensor", None),
            P(),
            P(),
            P(),
            P(),
            P(),
        ),
        check_vma=False,
    )
```

time: 705 us -> 553 us (0.78)
  waiting for transfers between devices: 311 us -> 183 us
  Pallas kernels: 33.3 us -> 157 us
  matrix products: 141 us -> 71.5 us
  starting transfers between devices: 98.6 us -> 42.5 us
  other arithmetic: 102 us -> 46.3 us
  local copies, waits for them, and re-layouts: 11.4 us -> 32.9 us
  between operations: 2.37 us -> 15.7 us
    pallas_call x0 -> x11, Pallas kernels: none -> 124 us  [the longest x2 41.4 us: forward(): pl.pallas_call(lambda *refs: forward_kernel(up_steps, *refs), out_shape=[...]
    ppermute x26 -> x2, waiting for transfers between devices: 119 us -> 2.99 us  [small_sum(): lax.ppermute(everywhere, 'tensor', [(i, i ^ reach) for i in range(size)])]
    ppermute x43 -> x57, waiting for transfers between devices: 193 us -> 85.2 us  [swap(): lax.ppermute(value, 'dp', [(i, i ^ 1 << bit) for i in range(self.size)])]
    all_gather x0 -> x4, waiting for transfers between devices: none -> 94.4 us  [the longest x1 48.8 us: shards(): top = lax.all_gather(tokens[:own_rows // 2], 'tensor', axis=0, tiled=True)]
    ppermute x26 -> x2, starting transfers between devices: 59.5 us -> 1.87 us  [small_sum(): lax.ppermute(everywhere, 'tensor', [(i, i ^ reach) for i in range(size)])]
    dot_general x4 -> x0, matrix products: 54.9 us -> none  [dot_nt(): lax.dot_general(a, b, (((1,), (1,)), ((), ())), preferred_element_type=F32)]
    convert_element_type x31 -> x16, other arithmetic: 52.1 us -> 16.5 us  [add(): (k.astype(F32) + g.astype(F32)).astype(BF16)]
    dot_general x4 -> x2, matrix products: 41.7 us -> 16 us  [dot_nn(): return jnp.dot(a, b, preferred_element_type=F32)]
  transfers between devices with their start and end apart: 69 -> 65, of which waited for: 32 -> 17; matrix products, arithmetic and copies ran while one was open for 33% -> 21% of each run, Pallas kernels for 5% -> 29%
where the time goes in v2:
time: 553 us; the launch traced here: 548 us
  waiting for transfers between devices  183 us (33%)
  Pallas kernels  157 us (28%)
  matrix products  71.5 us (13%)
  other arithmetic  46.3 us (8%)
  starting transfers between devices  42.5 us (8%)
  local copies, waits for them, and re-layouts  32.9 us (6%)
  between operations  15.7 us (3%)
    ppermute x57, waiting for transfers between devices, swap(): lax.ppermute(value, 'dp', [(i, i ^ 1 << bit) for i in range(self.size)])  85.2 us
    dot_general x12, matrix products, dot_tn(): lax.dot_general(a, b, (((0,), (0,)), ((), ())), preferred_element_type=F32)  55.5 us
    all_gather x1, waiting for transfers between devices, shards(): top = lax.all_gather(tokens[:own_rows // 2], 'tensor', axis=0, tiled=True)  48.8 us
    all_gather x1, waiting for transfers between devices, shards(): lax.all_gather(after(tokens[own_rows // 2:], top), 'tensor', axis=0, tile...  45.5 us
    pallas_call x2, Pallas kernels, forward(): pl.pallas_call(lambda *refs: forward_kernel(up_steps, *refs), out_shape=[...  41.4 us
    ppermute x57, starting transfers between devices, swap(): lax.ppermute(value, 'dp', [(i, i ^ 1 << bit) for i in range(self.size)])  40.4 us
    pallas_call x6, Pallas kernels, widen(): pl.pallas_call(lambda *refs: widen_kernel(rows, offset, column, *refs), o...  38.5 us
    pallas_call x1, Pallas kernels, inner_grad(): pl.pallas_call(inner_kernel, out_shape=(jax.ShapeDtypeStruct((group, widt...  23.7 us
  transfers between devices with their start and end apart: 65, of which 17 were waited for; matrix products, arithmetic and copies ran while one was open for 21% of the time, Pallas kernels for 29%

profile of v2, /device:TPU:0, one launch (start us, length us, event | category | flops | bytes accessed | tf_op | source)
XLA Modules:
  0.0 548.4 jit_solution(3811310331361824795)
XLA Ops:
  9.7 48.8 %all-gather.5.cloned.1.call-done.refs_0_ = bf16[512,2048]{1,0:T(8,128)(2,1)} async-done(((bf16[128,2048]{1,0:T(8,128)(2,1)}), bf16[512,2048]{1,0:T(8,128)(2,1)}) %all-gather.5.cloned.1.call-update) | async-done | bytes 2097168 | tf_op jit(solution)/shard_map/all_gather | solution.py:691
  59.7 45.5 %all-gather.7.cloned.1.call-done.refs_0_ = bf16[512,2048]{1,0:T(8,128)(2,1)} async-done(((bf16[128,2048]{1,0:T(8,128)(2,1)}), bf16[512,2048]{1,0:T(8,128)(2,1)}) %all-gather.7.cloned.1.call-update) | async-done | bytes 2097168 | tf_op jit(solution)/shard_map/all_gather | solution.py:692
  114.5 20.8 %forward.2 = (bf16[4,2,128,2048]{3,2,1,0:T(8,128)(2,1)}, bf16[4,2,128,2048]{3,2,1,0:T(8,128)(2,1)}, bf16[4,2,128,2048]{3,2,1,0:T(8,128)(2,1)}, f32[4,2,128,1]{3,...) custom-call(bf16[512,2048]{1,0:T(8,128)(2,1)} %all-gather.5.cloned.1, ...), custom_call_target="tpu_custom_call" | custom-call | tf_op jit(solution)/shard_map/forward/pallas_call | solution.py:306
  135.3 20.6 %forward.3 = (bf16[4,2,128,2048]{3,2,1,0:T(8,128)(2,1)}, bf16[4,2,128,2048]{3,2,1,0:T(8,128)(2,1)}, bf16[4,2,128,2048]{3,2,1,0:T(8,128)(2,1)}, f32[4,2,128,1]{3,...) custom-call(bf16[512,2048]{1,0:T(8,128)(2,1)} %all-gather.7.cloned.1, ...), custom_call_target="tpu_custom_call", output_to_operand_aliasing={{0}: (9, {}), {1}: (10, {}), {2}: (11, {}), {3}: (12, {}), ... | custom-call | tf_op jit(solution)/shard_map/forward/pallas_call | solution.py:306
  155.9 15.2 %attend.1 = (bf16[1024,1536]{1,0:T(8,128)(2,1)}, bf16[1024,512]{1,0:T(8,128)(2,1)}) custom-call(f32[1024,1536]{1,0:T(8,128)} %bitcast.46, f32[1024,128]{1,0:T(8,128)} %get-tuple-element.478.refs_1_.refs_2_, f32[1024,128]{1,0:T(8,128)} %concatenate.85.refs_2_.refs_3_, f32[1024,128]{1,0:T(8,128)} %get-tuple-element.479.refs_3_.refs_4_, s32[1024,1]{1,0:T(8,128)} %copy.42.refs_4_), custom_call_target="tpu_custom_call" | custom-call | tf_op jit(solution)/shard_map/attend/pallas_call | solution.py:108
  171.2 6.1 %fusion.22 = bf16[1024,1024]{1,0:T(8,128)(2,1)} fusion(bf16[1024,1024]{1,0:T(8,128)(2,1)} %all-gather.9.cloned.1.call-done.refs_0_, bf16[1024,2048]{1,0:T(8,128)(2,1)} %bitcast.53, s32[]{:T(128)S(6)} %select_n.220), kind=kOutput, calls=%fused_computation.39 | convolution fusion | flops 2148532224 | bytes 6291460 | tf_op jit(solution)/shard_map/dot_general | solution.py:66
  182.5 4.6 add_convert_fusion.4
  195.3 11.7 %fusion.66 = f32[1024,2048]{1,0:T(8,128)S(1)} fusion(bf16[1024,2048]{1,0:T(8,128)(2,1)S(1)} %bitcast.56, bf16[2048,2048]{1,0:T(8,128)(2,1)} %refs_2_.2), kind=kOutput, calls=%fused_computation.197 | convolution fusion | flops 8589934592 | bytes 20971520 | tf_op jit(solution)/shard_map/dot_general | solution.py:70
  207.0 4.4 add_convert_fusion.1
  217.2 7.6 %collective-permute-done.4 = bf16[160,1024]{1,0:T(8,128)(2,1)S(1)} collective-permute-done((bf16[160,1024]{1,0:T(8,128)(2,1)S(1)}, bf16[160,1024]{1,0:T(8,128)(2,1)S(1)}, u32[]{:S(2)}, u32[]{:S(2)}) %collective-permute-start.4) | collective-permute-done | bytes 327712 | tf_op jit(solution)/shard_map/ppermute | solution.py:534
  226.4 6.1 %fusion.25 = bf16[1024,1024]{1,0:T(8,128)(2,1)} fusion(bf16[1024,1024]{1,0:T(8,128)(2,1)} %all-gather.11.cloned.1.call-done.refs_1_, bf16[1024,2048]{1,0:T(8,128)(2,1)} %bitcast.55, s32[]{:T(128)S(6)} %select_n.220), kind=kOutput, calls=%fused_computation.40 | convolution fusion | flops 2148532224 | bytes 6291460 | tf_op jit(solution)/shard_map/dot_general | solution.py:66
  236.3 6.6 %collective-permute-done.6 = bf16[160,1024]{1,0:T(8,128)(2,1)} collective-permute-done((bf16[160,1024]{1,0:T(8,128)(2,1)}, bf16[160,1024]{1,0:T(8,128)(2,1)}, u32[]{:S(2)}, u32[]{:S(2)}) %collective-permute-start.6) | collective-permute-done | bytes 327712 | tf_op jit(solution)/shard_map/ppermute | solution.py:534
  251.0 4.0 add_convert_fusion.3
  257.2 14.4 %hidden_back.1 = (bf16[1024,2048]{1,0:T(8,128)(2,1)}, f32[8,2048]{1,0:T(8,128)}) custom-call(bf16[1024,1024]{1,0:T(8,128)(2,1)} %all-gather.9.cloned.1.call-done.refs_0_, bf16[1024,1024]{1,0:T(8,128)(2,1)} %all-gather.11.cloned.1.call-done.refs_1_, bf16[2048,2048]{1,0:T(8,128)(2,1)} %refs_2_.2, bf16[1024,2048]{1,0:T(8,128)(2,1)} %bitcast.48), custom_call_target="tpu_custom_call" | custom-call | tf_op jit(solution)/shard_map/hidden_back/pallas_call | solution.py:381
  271.6 7.5 %convolution_convert_fusion.1 = bf16[1024,2048]{1,0:T(8,128)(2,1)S(1)} fusion(bf16[1024,2048]{1,0:T(8,128)(2,1)} %get-tuple-element.299.hidden_ref, bf16[1024,2048]{1,0:T(8,128)(2,1)} %bitcast.51, s32[]{:T(128)S(6)} %select_n.220), kind=kOutput, calls=%fused_computation.6 | convolution fusion | flops 4297064448 | bytes 10485764 | tf_op jit(solution)/shard_map/dot_general | solution.py:66
  281.9 14.5 %collective-permute-done.17 = bf16[320,1024]{1,0:T(8,128)(2,1)S(1)} collective-permute-done((bf16[320,1024]{1,0:T(8,128)(2,1)S(1)}, bf16[320,1024]{1,0:T(8,128)(2,1)S(1)}, u32[]{:S(2)}, u32[]{:S(2)}) %collective-permute-start.17) | collective-permute-done | bytes 655392 | tf_op jit(solution)/shard_map/ppermute | solution.py:534
  301.6 5.1 add_convert_fusion
  310.9 5.9 %context_back.1.refs_1_ = bf16[1024,512]{1,0:T(8,128)(2,1)} custom-call(bf16[1024,1024]{1,0:T(8,128)(2,1)} %all-gather.9.cloned.1.call-done.refs_0_, bf16[1024,1024]{1,0:T(8,128)(2,1)} %all-gather.11.cloned.1.call-done.refs_1_, bf16[512,2048]{1,0:T(8,128)(2,1)} %refs_2_.3), custom_call_target="tpu_custom_call" | custom-call | tf_op jit(solution)/shard_map/context_back/pallas_call | solution.py:381
  321.4 17.6 %attend_back.1 = (bf16[1024,1536]{1,0:T(8,128)(2,1)}, f32[8,1536]{1,0:T(8,128)}) custom-call(bf16[1024,1536]{1,0:T(8,128)(2,1)} %get-tuple-element.288.refs_0_, bf16[1024,512]{1,0:T(8,128)(2,1)} %context_back.1.refs_1_, f32[1024,128]{1,0:T(8,128)} %get-tuple-element.478.refs_1_.refs_2_, f32[1024,128]{1,0:T(8,128)} %concatenate.85.refs_2_.refs_3_, ...), custom_call_target="tpu_custom_call" | custom-call | tf_op jit(solution)/shard_map/attend_back/pallas_call | solution.py:209
  342.2 9.5 %collective-permute-done.19 = bf16[256,2048]{1,0:T(8,128)(2,1)} collective-permute-done((bf16[256,2048]{1,0:T(8,128)(2,1)}, bf16[256,2048]{1,0:T(8,128)(2,1)}, u32[]{:S(2)}, u32[]{:S(2)}) %collective-permute-start.19) | collective-permute-done | bytes 1048608 | tf_op jit(solution)/shard_map/ppermute | solution.py:534
  358.8 23.7 %inner_grad.1 = (bf16[1024,2048]{1,0:T(8,128)(2,1)}, f32[4,2048]{1,0:T(4,128)}) custom-call(bf16[1024,2048]{1,0:T(8,128)(2,1)} %get-tuple-element.299.hidden_ref, bf16[2048,2048]{1,0:T(8,128)(2,1)} %up_ref.1, bf16[1024,1536]{1,0:T(8,128)(2,1)} %get-tuple-element.310.mixed_ref, bf16[2048,1536]{1,0:T(8,128)(2,1)} %qkv_ref.1, bf16[1024,2048]{1,0:T(8,128)(2,1)} %bitcast.47, ...), custom_call_target="tpu_custom_call" | custom-call | tf_op jit(solution)/shard_map/inner_grad/pallas_call | solution.py:429
  386.6 7.0 %convolution_convert_fusion = bf16[1024,1536]{1,0:T(8,128)(2,1)} fusion(bf16[1024,1536]{1,0:T(8,128)(2,1)S(1)} %copy-done.24, bf16[1024,2048]{1,0:T(8,128)(2,1)} %bitcast.49, s32[]{:T(128)S(6)} %select_n.220), kind=kOutput, calls=%fused_computation.5 | convolution fusion | flops 3222798336 | bytes 8388612 | tf_op jit(solution)/shard_map/dot_general | solution.py:66
  400.9 7.7 %add_convert_fusion.2 = bf16[1024,1536]{1,0:T(8,128)(2,1)S(1)} fusion(bf16[1024,1536]{1,0:T(8,128)(2,1)} %collective-permute-done.31, bf16[1024,1536]{1,0:T(8,128)(2,1)} %get-tuple-element.310.mixed_ref, bf16[1024,2048]{1,0:T(8,128)(2,1)} %bitcast.50, s32[]{:T(128)S(6)} %select_n.222), kind=kOutput, calls=%fused_computation.2 | convolution fusion | flops 3225944064 | bytes 11534340 | tf_op jit(solution)/shard_map/dot_general | solution.py:66
  421.2 6.3 %widen.6.refs_9_ = f32[2048,2048]{1,0:T(8,128)} custom-call(s32[3]{0:T(128)} %pad_add_fusion.refs_0_, bf16[320,1024]{1,0:T(8,128)(2,1)} %pad_maximum_fusion.6.refs_1_, bf16[320,1024]{1,0:T(8,128)(2,1)} %collective-permute-done.8.refs_2_, bf16[320,1024]{1,0:T(8,128)(2,1)} %pad_maximum_fusion.7.refs_3_, bf16[320,1024]{1,0:T(8,128)(2,1)} %collective-permute-done.9.refs_4_, ...), custom_call_target="tpu_custom_call" | custom-call | tf_op jit(solution)/shard_map/widen/pallas_call | solution.py:483
  427.5 4.7 widen.7.refs_9_
  434.3 6.3 %widen.8 = f32[2048,2048]{1,0:T(8,128)} custom-call(s32[3]{0:T(128)} %pad_add_fusion.refs_0_, bf16[320,1024]{1,0:T(8,128)(2,1)} %copy-done.11, bf16[320,1024]{1,0:T(8,128)(2,1)} %collective-permute-done.27.refs_2_, bf16[320,1024]{1,0:T(8,128)(2,1)} %copy-done.12, bf16[320,1024]{1,0:T(8,128)(2,1)} %collective-permute-done.28.refs_4_, ...), custom_call_target="tpu_custom_call", output_to_operand_aliasing={{}: (9, {})} | custom-call | tf_op jit(solution)/shard_map/widen/pallas_call | solution.py:483
  453.4 4.7 widen.9
  466.8 21.6 %collective-permute-done.44 = f32[1,13824]{1,0:T(1,128)S(1)} collective-permute-done((f32[1,13824]{1,0:T(1,128)S(1)}, f32[1,13824]{1,0:T(1,128)S(1)}, u32[]{:S(2)}, u32[]{:S(2)}) %collective-permute-start.44) | collective-permute-done | bytes 55328 | tf_op jit(solution)/shard_map/ppermute | solution.py:534
  496.7 13.8 %collective-permute-done.47.refs_2_ = bf16[256,1536]{1,0:T(8,128)(2,1)} collective-permute-done((bf16[256,1536]{1,0:T(8,128)(2,1)}, bf16[256,1536]{1,0:T(8,128)(2,1)}, u32[]{:S(2)}, u32[]{:S(2)}) %collective-permute-start.47) | collective-permute-done | bytes 786464 | tf_op jit(solution)/shard_map/ppermute | solution.py:534
  510.5 3.1 collective-permute-done.48.refs_4_
  513.5 9.1 %widen.10 = f32[2048,2048]{1,0:T(8,128)} custom-call(s32[3]{0:T(128)} %pad_add_fusion.refs_0_, bf16[256,2048]{1,0:T(8,128)(2,1)} %pad_maximum_fusion.refs_1_, bf16[256,2048]{1,0:T(8,128)(2,1)} %collective-permute-done.45.refs_2_, bf16[256,2048]{1,0:T(8,128)(2,1)} %pad_maximum_fusion.1.refs_3_, bf16[256,2048]{1,0:T(8,128)(2,1)} %collective-permute-done.46.refs_4_, ...), custom_call_target="tpu_custom_call" | custom-call | tf_op jit(solution)/shard_map/widen/pallas_call | solution.py:483
  529.1 7.4 %widen.11 = f32[2048,1536]{1,0:T(8,128)} custom-call(s32[3]{0:T(128)} %pad_add_fusion.refs_0_, bf16[256,1536]{1,0:T(8,128)(2,1)} %pad_maximum_fusion.2.refs_1_, bf16[256,1536]{1,0:T(8,128)(2,1)} %collective-permute-done.47.refs_2_, bf16[256,1536]{1,0:T(8,128)(2,1)} %pad_maximum_fusion.3.refs_3_, bf16[256,1536]{1,0:T(8,128)(2,1)} %copy-done.33, ...), custom_call_target="tpu_custom_call" | custom-call | tf_op jit(solution)/shard_map/widen/pallas_call | solution.py:483
  (376 shorter events, 140.6 us)
Async XLA Ops:
  7.2 51.4 %all-gather.5.cloned.1.call-start = ((), (), s32[]{:S(2)}) async-start(), calls=%async_computation.2 | async-start | bytes 2621440 | tf_op jit(solution)/shard_map/all_gather | solution.py:691
  9.7 95.5 %all-gather.7.cloned.1.call-start = ((), (), s32[]{:S(2)}) async-start(), calls=%async_computation.3 | async-start | bytes 2621440 | tf_op jit(solution)/shard_map/all_gather | solution.py:692
  58.6 112.6 %all-gather.9.cloned.1.call-start = ((), (), s32[]{:S(2)}) async-start(), calls=%async_computation.4 | async-start | bytes 2621440 | tf_op jit(solution)/shard_map/all_gather | solution.py:693
  105.2 121.2 %all-gather.11.cloned.1.call-start = ((), (), s32[]{:S(2)}) async-start(), calls=%async_computation.5 | async-start | bytes 2621440 | tf_op jit(solution)/shard_map/all_gather | solution.py:694
  180.3 277.8 %reduce-scatter.3.cloned.1.call-start = ((), (), s32[]{:S(2)}) async-start(), calls=%async_computation.6 | async-start | bytes 5242880 | tf_op jit(solution)/shard_map/reduce_scatter | solution.py:724
  191.3 20.0 %collective-permute-start.2 = (bf16[320,1024]{1,0:T(8,128)(2,1)}, bf16[320,1024]{1,0:T(8,128)(2,1)}, u32[]{:S(2)}, u32[]{:S(2)}) collective-permute-start(bf16[320,1024]{1,0:T(8,128)(2,1)} %pad_maximum_fusion.4), channel_id=1, source_target_pairs={{0,8},{4,12},{8,0},{12,4},{16,24},{20,28},{24,16},{28,20},{1,9},{5... | collective-permute-start | bytes 1966088 | tf_op jit(solution)/shard_map/ppermute | solution.py:534
  246.8 24.8 %collective-permute-start.8 = (bf16[320,1024]{1,0:T(8,128)(2,1)}, bf16[320,1024]{1,0:T(8,128)(2,1)}, u32[]{:S(2)}, u32[]{:S(2)}) collective-permute-start(bf16[320,1024]{1,0:T(8,128)(2,1)} %pad_maximum_fusion.6.refs_1_), channel_id=1, source_target_pairs={{0,8},{4,12},{8,0},{12,4},{16,24},{20,28},{24,16},{28,20},{1,9},{5... | collective-permute-start | bytes 1966088 | tf_op jit(solution)/shard_map/ppermute | solution.py:534
  250.2 21.4 %collective-permute-start.9 = (bf16[320,1024]{1,0:T(8,128)(2,1)}, bf16[320,1024]{1,0:T(8,128)(2,1)}, u32[]{:S(2)}, u32[]{:S(2)}) collective-permute-start(bf16[320,1024]{1,0:T(8,128)(2,1)} %pad_maximum_fusion.7.refs_3_), channel_id=1, source_target_pairs={{0,16},{4,20},{8,24},{12,28},{16,0},{20,4},{24,8},{28,12},{1,17},{... | collective-permute-start | bytes 1966088 | tf_op jit(solution)/shard_map/ppermute | solution.py:534
  279.2 21.5 %collective-permute-start.16 = (bf16[1024,2048]{1,0:T(8,128)(2,1)S(1)}, bf16[1024,2048]{1,0:T(8,128)(2,1)S(1)}, u32[]{:S(2)}, u32[]{:S(2)}) collective-permute-start(bf16[1024,2048]{1,0:T(8,128)(2,1)S(1)} %convolution_convert_fusion.1), channel_id=1, source_target_pairs={{0,4},{4,0},{8,12},{12,8},{16,20},{20,16},{24,28},{28,24},{1,5},{5... | collective-permute-start | bytes 12582920 | tf_op jit(solution)/shard_map/ppermute | solution.py:534
  316.9 22.9 %collective-permute-start.23 = (bf16[160,1024]{1,0:T(8,128)(2,1)S(1)}, bf16[160,1024]{1,0:T(8,128)(2,1)S(1)}, u32[]{:S(2)}, u32[]{:S(2)}) collective-permute-start(bf16[160,1024]{1,0:T(8,128)(2,1)S(1)} %add_convert_fusion.18), channel_id=1, source_target_pairs={{0,16},{4,20},{8,24},{12,28},{16,0},{20,4},{24,8},{28,12},{1,17},{... | collective-permute-start | bytes 983048 | tf_op jit(solution)/shard_map/ppermute | solution.py:534
  318.5 21.4 %collective-permute-start.24 = (bf16[160,1024]{1,0:T(8,128)(2,1)S(1)}, bf16[160,1024]{1,0:T(8,128)(2,1)S(1)}, u32[]{:S(2)}, u32[]{:S(2)}) collective-permute-start(bf16[160,1024]{1,0:T(8,128)(2,1)S(1)} %add_convert_fusion.17), channel_id=1, source_target_pairs={{0,8},{4,12},{8,0},{12,4},{16,24},{20,28},{24,16},{28,20},{1,9},{5... | collective-permute-start | bytes 983048 | tf_op jit(solution)/shard_map/ppermute | solution.py:534
  319.2 217.4 %reduce-scatter.5.cloned.1.call-start = ((), (), s32[]{:S(2)}) async-start(), calls=%async_computation.7 | async-start | bytes 5242880 | tf_op jit(solution)/shard_map/reduce_scatter | solution.py:755
  319.2 32.5 %collective-permute-start.19 = (bf16[256,2048]{1,0:T(8,128)(2,1)}, bf16[256,2048]{1,0:T(8,128)(2,1)}, u32[]{:S(2)}, u32[]{:S(2)}) collective-permute-start(bf16[256,2048]{1,0:T(8,128)(2,1)} %constant_dynamic-slice_fusion.11), channel_id=1, source_target_pairs={{0,8},{4,12},{8,0},{12,4},{16,24},{20,28},{24,16},{28,20},{1,9},{5... | collective-permute-start | bytes 3145736 | tf_op jit(solution)/shard_map/ppermute | solution.py:534
  320.7 31.0 %collective-permute-start.20 = (bf16[256,2048]{1,0:T(8,128)(2,1)}, bf16[256,2048]{1,0:T(8,128)(2,1)}, u32[]{:S(2)}, u32[]{:S(2)}) collective-permute-start(bf16[256,2048]{1,0:T(8,128)(2,1)} %constant_dynamic-slice_fusion.10), channel_id=1, source_target_pairs={{0,16},{4,20},{8,24},{12,28},{16,0},{20,4},{24,8},{28,12},{1,17},{... | collective-permute-start | bytes 3145736 | tf_op jit(solution)/shard_map/ppermute | solution.py:534
  340.0 42.5 %collective-permute-start.27 = (bf16[320,1024]{1,0:T(8,128)(2,1)S(1)}, bf16[320,1024]{1,0:T(8,128)(2,1)}, u32[]{:S(2)}, u32[]{:S(2)}) collective-permute-start(bf16[320,1024]{1,0:T(8,128)(2,1)S(1)} %pad_maximum_fusion.10.refs_1_), channel_id=1, source_target_pairs={{0,8},{4,12},{8,0},{12,4},{16,24},{20,28},{24,16},{28,20},{1,9},{5... | collective-permute-start | bytes 1966088 | tf_op jit(solution)/shard_map/ppermute | solution.py:534
  341.0 41.5 %collective-permute-start.28 = (bf16[320,1024]{1,0:T(8,128)(2,1)S(1)}, bf16[320,1024]{1,0:T(8,128)(2,1)}, u32[]{:S(2)}, u32[]{:S(2)}) collective-permute-start(bf16[320,1024]{1,0:T(8,128)(2,1)S(1)} %pad_maximum_fusion.11.refs_3_), channel_id=1, source_target_pairs={{0,16},{4,20},{8,24},{12,28},{16,0},{20,4},{24,8},{28,12},{1,17},{... | collective-permute-start | bytes 1966088 | tf_op jit(solution)/shard_map/ppermute | solution.py:534
  354.8 27.7 %collective-permute-start.25 = (bf16[128,2048]{1,0:T(8,128)(2,1)}, bf16[128,2048]{1,0:T(8,128)(2,1)}, u32[]{:S(2)}, u32[]{:S(2)}) collective-permute-start(bf16[128,2048]{1,0:T(8,128)(2,1)} %get-tuple-element.416), channel_id=1, source_target_pairs={{0,16},{4,20},{8,24},{12,28},{16,0},{20,4},{24,8},{28,12},{1,17},{... | collective-permute-start | bytes 1572872 | tf_op jit(solution)/shard_map/ppermute | solution.py:534
  358.0 24.5 %collective-permute-start.26 = (bf16[128,2048]{1,0:T(8,128)(2,1)}, bf16[128,2048]{1,0:T(8,128)(2,1)}, u32[]{:S(2)}, u32[]{:S(2)}) collective-permute-start(bf16[128,2048]{1,0:T(8,128)(2,1)} %get-tuple-element.414), channel_id=1, source_target_pairs={{0,8},{4,12},{8,0},{12,4},{16,24},{20,28},{24,16},{28,20},{1,9},{5... | collective-permute-start | bytes 1572872 | tf_op jit(solution)/shard_map/ppermute | solution.py:534
  394.8 19.2 %collective-permute-start.10 = (bf16[320,1024]{1,0:T(8,128)(2,1)}, bf16[320,1024]{1,0:T(8,128)(2,1)}, u32[]{:S(2)}, u32[]{:S(2)}) collective-permute-start(bf16[320,1024]{1,0:T(8,128)(2,1)} %pad_maximum_fusion.6.refs_1_), channel_id=1, source_target_pairs={{0,4},{4,0},{8,12},{12,8},{16,20},{20,16},{24,28},{28,24},{1,5},{5... | collective-permute-start | bytes 1966088 | tf_op jit(solution)/shard_map/ppermute | solution.py:534
  395.3 19.2 %collective-permute-start.12 = (bf16[320,1024]{1,0:T(8,128)(2,1)}, bf16[320,1024]{1,0:T(8,128)(2,1)}, u32[]{:S(2)}, u32[]{:S(2)}) collective-permute-start(bf16[320,1024]{1,0:T(8,128)(2,1)} %pad_maximum_fusion.7.refs_3_), channel_id=1, source_target_pairs={{0,4},{4,0},{8,12},{12,8},{16,20},{20,16},{24,28},{28,24},{1,5},{5... | collective-permute-start | bytes 1966088 | tf_op jit(solution)/shard_map/ppermute | solution.py:534
  395.4 20.4 %collective-permute-start.11 = (bf16[320,1024]{1,0:T(8,128)(2,1)}, bf16[320,1024]{1,0:T(8,128)(2,1)}, u32[]{:S(2)}, u32[]{:S(2)}) collective-permute-start(bf16[320,1024]{1,0:T(8,128)(2,1)} %collective-permute-done.8.refs_2_), channel_id=1, source_target_pairs={{0,4},{4,0},{8,12},{12,8},{16,20},{20,16},{24,28},{28,24},{1,5},{5... | collective-permute-start | bytes 1966088 | tf_op jit(solution)/shard_map/ppermute | solution.py:534
  414.6 26.1 %collective-permute-start.38 = (bf16[256,1536]{1,0:T(8,128)(2,1)}, bf16[256,1536]{1,0:T(8,128)(2,1)}, u32[]{:S(2)}, u32[]{:S(2)}) collective-permute-start(bf16[256,1536]{1,0:T(8,128)(2,1)} %constant_dynamic-slice_fusion.5), channel_id=1, source_target_pairs={{0,8},{4,12},{8,0},{12,4},{16,24},{20,28},{24,16},{28,20},{1,9},{5... | collective-permute-start | bytes 2359304 | tf_op jit(solution)/shard_map/ppermute | solution.py:534
  415.8 24.9 %collective-permute-start.39 = (bf16[256,1536]{1,0:T(8,128)(2,1)}, bf16[256,1536]{1,0:T(8,128)(2,1)}, u32[]{:S(2)}, u32[]{:S(2)}) collective-permute-start(bf16[256,1536]{1,0:T(8,128)(2,1)} %constant_dynamic-slice_fusion.4), channel_id=1, source_target_pairs={{0,16},{4,20},{8,24},{12,28},{16,0},{20,4},{24,8},{28,12},{1,17},{... | collective-permute-start | bytes 2359304 | tf_op jit(solution)/shard_map/ppermute | solution.py:534
  449.8 38.6 %collective-permute-start.45 = (bf16[256,2048]{1,0:T(8,128)(2,1)S(1)}, bf16[256,2048]{1,0:T(8,128)(2,1)}, u32[]{:S(2)}, u32[]{:S(2)}) collective-permute-start(bf16[256,2048]{1,0:T(8,128)(2,1)S(1)} %copy-done.19), channel_id=1, source_target_pairs={{0,8},{4,12},{8,0},{12,4},{16,24},{20,28},{24,16},{28,20},{1,9},{5... | collective-permute-start | bytes 3145736 | tf_op jit(solution)/shard_map/ppermute | solution.py:534
  450.7 38.2 %collective-permute-start.46 = (bf16[256,2048]{1,0:T(8,128)(2,1)}, bf16[256,2048]{1,0:T(8,128)(2,1)}, u32[]{:S(2)}, u32[]{:S(2)}) collective-permute-start(bf16[256,2048]{1,0:T(8,128)(2,1)} %pad_maximum_fusion.1.refs_3_), channel_id=1, source_target_pairs={{0,16},{4,20},{8,24},{12,28},{16,0},{20,4},{24,8},{28,12},{1,17},{... | collective-permute-start | bytes 3145736 | tf_op jit(solution)/shard_map/ppermute | solution.py:534
  462.1 27.0 %collective-permute-start.42 = (bf16[128,1536]{1,0:T(8,128)(2,1)S(1)}, bf16[128,1536]{1,0:T(8,128)(2,1)S(1)}, u32[]{:S(2)}, u32[]{:S(2)}) collective-permute-start(bf16[128,1536]{1,0:T(8,128)(2,1)S(1)} %add_convert_fusion.16), channel_id=1, source_target_pairs={{0,16},{4,20},{8,24},{12,28},{16,0},{20,4},{24,8},{28,12},{1,17},{... | collective-permute-start | bytes 1179656 | tf_op jit(solution)/shard_map/ppermute | solution.py:534
  464.1 26.0 %collective-permute-start.43 = (bf16[128,1536]{1,0:T(8,128)(2,1)S(1)}, bf16[128,1536]{1,0:T(8,128)(2,1)S(1)}, u32[]{:S(2)}, u32[]{:S(2)}) collective-permute-start(bf16[128,1536]{1,0:T(8,128)(2,1)S(1)} %add_convert_fusion.15), channel_id=1, source_target_pairs={{0,8},{4,12},{8,0},{12,4},{16,24},{20,28},{24,16},{28,20},{1,9},{5... | collective-permute-start | bytes 1179656 | tf_op jit(solution)/shard_map/ppermute | solution.py:534
  465.4 23.0 %collective-permute-start.44 = (f32[1,13824]{1,0:T(1,128)S(1)}, f32[1,13824]{1,0:T(1,128)S(1)}, u32[]{:S(2)}, u32[]{:S(2)}) collective-permute-start(f32[1,13824]{1,0:T(1,128)S(1)} %copy-done.34), channel_id=1, source_target_pairs={{0,16},{4,20},{8,24},{12,28},{16,0},{20,4},{24,8},{28,12},{1,17},{... | collective-permute-start | bytes 165896 | tf_op jit(solution)/shard_map/ppermute | solution.py:534
  491.1 19.3 %collective-permute-start.47 = (bf16[256,1536]{1,0:T(8,128)(2,1)}, bf16[256,1536]{1,0:T(8,128)(2,1)}, u32[]{:S(2)}, u32[]{:S(2)}) collective-permute-start(bf16[256,1536]{1,0:T(8,128)(2,1)} %pad_maximum_fusion.2.refs_1_), channel_id=1, source_target_pairs={{0,8},{4,12},{8,0},{12,4},{16,24},{20,28},{24,16},{28,20},{1,9},{5... | collective-permute-start | bytes 2359304 | tf_op jit(solution)/shard_map/ppermute | solution.py:534
  495.8 26.9 %collective-permute-start.53 = (f32[1,10240]{1,0:T(1,128)S(1)}, f32[1,10240]{1,0:T(1,128)S(1)}, u32[]{:S(2)}, u32[]{:S(2)}) collective-permute-start(f32[1,10240]{1,0:T(1,128)S(1)} %slice.287), channel_id=1, source_target_pairs={{0,1},{1,0},{2,3},{3,2},{4,5},{5,4},{6,7},{7,6},{8,9},{9,8},{10,11... | collective-permute-start | bytes 122888 | tf_op jit(solution)/shard_map/ppermute | solution.py:658
  496.2 32.8 %collective-permute-start.49 = (bf16[256,1536]{1,0:T(8,128)(2,1)}, bf16[256,1536]{1,0:T(8,128)(2,1)}, u32[]{:S(2)}, u32[]{:S(2)}) collective-permute-start(bf16[256,1536]{1,0:T(8,128)(2,1)} %pad_maximum_fusion.2.refs_1_), channel_id=1, source_target_pairs={{0,4},{4,0},{8,12},{12,8},{16,20},{20,16},{24,28},{28,24},{1,5},{5... | collective-permute-start | bytes 2359304 | tf_op jit(solution)/shard_map/ppermute | solution.py:534
  496.2 32.8 %collective-permute-start.51 = (bf16[256,1536]{1,0:T(8,128)(2,1)}, bf16[256,1536]{1,0:T(8,128)(2,1)}, u32[]{:S(2)}, u32[]{:S(2)}) collective-permute-start(bf16[256,1536]{1,0:T(8,128)(2,1)} %pad_maximum_fusion.3.refs_3_), channel_id=1, source_target_pairs={{0,4},{4,0},{8,12},{12,8},{16,20},{20,16},{24,28},{28,24},{1,5},{5... | collective-permute-start | bytes 2359304 | tf_op jit(solution)/shard_map/ppermute | solution.py:534
  (81 other events, 1506.9 us)
Sparse Core Ops, SparseCore 0:
  10.1 48.3 all-gather.4
  60.7 44.4 all-gather.6
  106.8 44.4 all-gather.8
  180.5 44.7 all-gather.10
  319.3 74.9 reduce-scatter.2
  396.9 76.8 reduce-scatter.4
